TPU v7x, 32 devices: a whole 2x2x4 slice. The times are simulated.
32 devices in a mesh: slab: 16 (over z, y, x), pencil: 2 (over core).
Axes of the slice: x: 2, y: 2, z: 4, core: 2. Of those that a mesh axis runs over, the one named last changes fastest.
Arguments:
- owner_map: int32 [16], replicated, may hold values from 0 to 15
- window_start: int32 [1], replicated, may hold values from 0 to 8
- child_maps: float32 [8, 20, 20], replicated, may hold values from -1 to 1
- innovation: float32 [20, 20], replicated, may hold values from -1.25 to 1.25
- coarse_bank: float32 [16, 20, 74898], P('slab'), may hold values from -6 to 6
- noise_middle: float32 [20, 64, 64, 128], P(None, 'slab', 'pencil'), may hold values from -6 to 6
- noise_finest: float32 [20, 128, 128, 256], P(None, 'slab', 'pencil'), may hold values from -6 to 6
Outputs:
- field_values: float32 [256, 256, 512], P('slab', 'pencil')
- zface_mean: float32 [128, 256, 512], P('slab', 'pencil')
- yface_mean: float32 [256, 128, 512], P('slab', 'pencil')
All inputs are finite; a program needn't handle non-finite values.
Results may differ from a plain program's by a relative error of at most 0.0001.
Values sent between devices are 32-bit elements; how exact they have to be, the bound alone decides.
A program may use at most 448 MiB of HBM per device.

v0:
```python
import math

import jax
import jax.numpy as jnp
import numpy as np
from jax import lax
from jax.sharding import PartitionSpec as P

LEVELS = 8
ROOTS = 2
ROOTS_Z = 1
ROOTS_Y = 1


def from_root(block, axis, owner):
    block = jnp.where(lax.axis_index(axis) == owner, block, jnp.zeros_like(block))
    return lax.psum(block, axis)


def shifted(block, axis, distance):
    devices = range(lax.axis_size(axis))
    route = [((i - distance) % len(devices), i) for i in devices]
    return lax.ppermute(block, axis, route)


def legendre(order, point):
    values = [1.0, point, 1.5 * point * point - 0.5, 2.5 * point * point * point - 1.5 * point]
    return values[order]


def basis_table(points):
    table_rows = []
    for point in points:
        w_coord, v_coord, u_coord = point
        entry = []
        for deg_x in range(4):
            for deg_y in range(4):
                for deg_z in range(4):
                    if deg_x + deg_y + deg_z <= 3:
                        factor = math.sqrt((2 * deg_x + 1) * (2 * deg_y + 1) * (2 * deg_z + 1))
                        entry.append(
                            factor
                            * legendre(deg_x, u_coord)
                            * legendre(deg_y, v_coord)
                            * legendre(deg_z, w_coord)
                        )
        table_rows.append(entry)
    return jnp.asarray(np.array(table_rows), jnp.float32)


def level_span(level):
    first = ROOTS_Z * ROOTS_Y * ROOTS
    return (first * (8**level - 1) // 7, first * 8**level)


def level_block(flat, level):
    scale = 2**level
    offset, length = level_span(level)
    return flat[:, offset : offset + length].reshape(
        flat.shape[0], ROOTS_Z * scale, ROOTS_Y * scale, ROOTS * scale
    )


def descend(parent, child_maps):
    kids = jnp.einsum("okn,nzyx->okzyx", child_maps, parent, precision=lax.Precision.HIGHEST)
    count, planes, rows_y, cols_x = parent.shape
    kids = kids.reshape(2, 2, 2, count, planes, rows_y, cols_x).transpose(3, 4, 0, 5, 1, 6, 2)
    return kids.reshape(count, 2 * planes, 2 * rows_y, 2 * cols_x)


def innovate(innovation, noise):
    return jnp.einsum("kn,nzyx->kzyx", innovation, noise, precision=lax.Precision.HIGHEST)


def expand(table, coeffs):
    return jnp.einsum("pk,kzyx->pzyx", table, coeffs, precision=lax.Precision.HIGHEST)


def refine(coeffs, child_maps, plane_start, planes, row_start, rows):
    zero = jnp.zeros((), jnp.int32)
    plane_start = jnp.asarray(plane_start, jnp.int32)
    row_start = jnp.asarray(row_start, jnp.int32)
    parent_start = plane_start // 2
    parent_row = row_start // 2
    parent_planes = max(1, planes // 2)
    parent_rows = max(1, rows // 2)
    count = coeffs.shape[0]
    parents = lax.dynamic_slice(
        coeffs,
        (zero, parent_start, parent_row, zero),
        (count, parent_planes, parent_rows, coeffs.shape[3]),
    )
    spread = descend(parents, child_maps)
    return lax.dynamic_slice(
        spread,
        (zero, plane_start - 2 * parent_start, row_start - 2 * parent_row, zero),
        (count, planes, rows, spread.shape[3]),
    )


def shards(
    owner_map, window_start, child_maps, innovation, coarse_bank, noise_middle, noise_finest
):
    bank_levels = LEVELS - 2
    last_level = bank_levels - 1
    local_bank = coarse_bank[0]
    owners = [owner_map[window_start[0] + level] for level in range(bank_levels)]
    position = lax.axis_index("slab")
    coeffs = None
    received = [
        from_root(level_block(local_bank, level), "slab", owners[level])
        for level in range(last_level)
    ]
    for level in range(last_level):
        fresh = innovate(innovation, received[level])
        coeffs = fresh if level == 0 else descend(coeffs, child_maps) + fresh
    count, planes, rows_y, cols_x = noise_middle.shape
    first_plane = position * planes
    first_row = lax.axis_index("pencil") * rows_y
    top_start = first_plane // 2
    top_row = first_row // 2
    top_planes = max(1, planes // 2)
    top_rows = max(1, rows_y // 2)
    scale = 2**last_level
    bank_cols = ROOTS * scale
    zero = jnp.zeros((), jnp.int32)
    whole_bank = from_root(level_block(local_bank, last_level), "slab", owners[last_level])
    noise_top = lax.dynamic_slice(
        whole_bank, (zero, top_start, top_row, zero), (count, top_planes, top_rows, bank_cols)
    )
    upper_level = refine(coeffs, child_maps, top_start, top_planes, top_row, top_rows) + innovate(
        innovation, noise_top
    )
    middle = refine(
        upper_level,
        child_maps,
        first_plane - 2 * top_start,
        planes,
        first_row - 2 * top_row,
        rows_y,
    ) + innovate(innovation, noise_middle)
    fine = descend(middle, child_maps) + innovate(innovation, noise_finest)
    count, fine_planes, fine_rows, fine_cols = fine.shape
    halves = [-0.5, 0.5]
    inner = basis_table([(pz, py, px) for pz in halves for py in halves for px in halves])
    top = basis_table([(1.0, py, px) for py in halves for px in halves])
    bottom = basis_table([(-1.0, py, px) for py in halves for px in halves])
    north = basis_table([(pz, 1.0, px) for pz in halves for px in halves])
    south = basis_table([(pz, -1.0, px) for pz in halves for px in halves])
    values = (
        expand(inner, fine)
        .reshape(2, 2, 2, fine_planes, fine_rows, fine_cols)
        .transpose(3, 0, 4, 1, 5, 2)
    )
    field_values = values.reshape(2 * fine_planes, 2 * fine_rows, 2 * fine_cols)
    lower_faces = expand(bottom, fine)
    south_faces = expand(south, fine)
    above_coeffs = shifted(fine[:, :1], "slab", -1)
    beside_coeffs = shifted(fine[:, :, :1], "pencil", -1)
    above = expand(bottom, above_coeffs)
    beside = expand(south, beside_coeffs)
    lower_next = jnp.concatenate([lower_faces[:, 1:], above], axis=1)
    south_next = jnp.concatenate([south_faces[:, :, 1:], beside], axis=2)
    zsum = expand(top, fine) + lower_next
    zface = (0.5 * zsum).reshape(2, 2, fine_planes, fine_rows, fine_cols).transpose(2, 3, 0, 4, 1)
    zface_mean = zface.reshape(fine_planes, 2 * fine_rows, 2 * fine_cols)
    ysum = expand(north, fine) + south_next
    yface = (0.5 * ysum).reshape(2, 2, fine_planes, fine_rows, fine_cols).transpose(2, 0, 3, 4, 1)
    yface_mean = yface.reshape(2 * fine_planes, fine_rows, 2 * fine_cols)
    return (field_values, zface_mean, yface_mean)


def solution(mesh):
    placed = (
        P(),
        P(),
        P(),
        P(),
        P("slab", None, None),
        P(None, "slab", "pencil", None),
        P(None, "slab", "pencil", None),
    )
    return jax.shard_map(
        shards,
        mesh=mesh,
        in_specs=placed,
        out_specs=(P("slab", "pencil", None), P("slab", "pencil", None), P("slab", "pencil", None)),
        check_vma=False,
    )
```

profile of v0, /device:TPU:0, one launch (start us, length us, event | category | flops | bytes accessed | tf_op | source)
XLA Modules:
  0.0 1258.6 jit_solution(5010336957763130200)
XLA Ops:
  11.5 26.7 %copy.91 = f32[1,20,74898]{1,2,0:T(8,128)} copy(f32[1,20,74898]{2,0,1:T(1,128)} %param.16) | data formatting | bytes 11983680 | tf_op args[4]
  40.1 4.6 slice_select_fusion.1
  44.7 22.8 %slice_select_fusion = f32[20,65536]{0,1:T(8,128)} fusion(f32[20,74898]{0,1:T(8,128)} %bitcast.227, pred[]{:T(512)S(6)} %eq.23), kind=kLoop, calls=%fused_computation | loop fusion | flops 1310720 | bytes 10485761 | tf_op jit(solution)/shard_map/jit(_where)/select_n | solution.py:16
  67.5 23.8 %copy.108 = f32[20,32,32,64]{3,0,2,1:T(8,128)} copy(f32[20,32,32,64]{0,3,2,1:T(8,128)} %bitcast.231) | data formatting | bytes 10485760 | tf_op jit(solution)/shard_map/jit(_where)/select_n | solution.py:16
  91.3 5.5 copy.103
  100.9 85.6 %all-reduce = (f32[20,2]{0,1:T(2,128)S(1)}, f32[20,2,2,4]{0,3,2,1:T(4,128)S(1)}, f32[20,4,4,8]{0,3,2,1:T(8,128)S(1)}) all-reduce(f32[20,2]{0,1:T(2,128)S(1)} %slice_select_fusion.5, f32[20,2,2,4]{0,3,2,1:T(4,128)S(1)} %bitcast.254, f32[20,4,4,8]{0,3,2,1:T(8,128)S(1)} %bitcast.252), channel_id=1, replica_groups=mesh['slab'=16,'pencil'=2] {'slab'}, use_global_device_ids=true, to_apply=%region_0.1 | all-reduce | flops 2920 | bytes 23360 | tf_op jit(solution)/shard_map/psum | solution.py:17
  192.5 348.9 %all-reduce.4.cloned.1.call-done = (f32[20,8,8,16]{0,3,2,1:T(8,128)}, f32[20,16,16,32]{3,0,2,1:T(8,128)}, f32[20,32,32,64]{3,0,2,1:T(8,128)}) async-done(((f32[20,8,8,16]{0,3,2,1:T(8,128)}, f32[20,16,16,32]{3,0,2,1:T(8,128)}, f32[20,32,32,64]{3,0,2,1:T(8,128)}), (f32[20,8,8,16]{0,3,2,1:T(8,128)}, f32[20,16,16,32]{3,0,2,1:T(8,128)}, f32[20,32,32,64]{3,0,2,1:T(8,128)})) %all-reduce.4.cloned.1.call-update) | async-done | bytes 5980176 | tf_op jit(solution)/shard_map/psum | solution.py:17
  541.4 6.4 convolution_bitcast_fusion
  563.4 12.3 copy.111
  575.7 5.2 copy.113
  581.0 13.9 %fusion.7 = f32[4,32,128,8,20]{2,4,3,1,0:T(8,128)} fusion(f32[20,4,32,128]{3,0,2,1:T(8,128)S(1)} %copy.113, f32[20,4,32,128]{3,0,2,1:T(8,128)} %fusion.12, f32[8,20,20,1,1]{2,0,1,4,3:T(8,128)S(1)} %bitcast.245), kind=kOutput, calls=%fused_computation.10 | convolution fusion | flops 629473280 | bytes 13120000 | tf_op jit(solution)/shard_map/okn,nzyx->okzyx/dot_general | solution.py:65
  594.8 78.5 %copy.115 = f32[2,2,2,20,4,32,128]{3,2,6,1,5,0,4:T(2,128)} copy(f32[2,2,2,20,4,32,128]{6,3,2,1,0,5,4:T(8,128)} %bitcast.233) | data formatting | bytes 20971520 | tf_op jit(solution)/shard_map/reshape | solution.py:67
  673.4 38.4 %copy.117 = f32[20,8,64,256]{3,0,2,1:T(8,128)} copy(f32[20,8,64,256]{0,3,2,1:T(8,128)} %bitcast.73) | data formatting | bytes 20971520 | tf_op jit(solution)/shard_map/reshape | solution.py:68
  711.8 23.1 %fusion.2 = f32[20,8,64,256]{3,0,2,1:T(8,128)S(1)} fusion(f32[20,8,64,256]{3,0,2,1:T(8,128)} %copy.117, f32[20,8,64,256]{3,2,1,0:T(8,128)} %param.18, f32[20,20]{1,0:T(8,128)S(1)} %copy-done.5), kind=kOutput, calls=%fused_computation.3 | convolution fusion | flops 631767040 | bytes 31458880 | tf_op jit(solution)/shard_map/kn,nzyx->kzyx/dot_general | solution.py:72
  740.6 7.7 fusion.50
  748.3 86.5 %fusion.52 = f32[4,8,63,256]{3,0,2,1:T(4,128)} fusion(f32[4,20,1,1]{1,0,3,2:T(4,128)S(1)} %copy-done.12, f32[20,8,64,256]{3,0,2,1:T(8,128)S(1)} %fusion.2), kind=kOutput, calls=%fused_computation.67 | convolution fusion | flops 123863040 | bytes 12550464 | tf_op jit(solution)/shard_map/slice | solution.py:163
  834.8 16.2 %fusion.51 = f32[4,7,64,256]{3,0,2,1:T(4,128)} fusion(f32[4,20,1,1]{1,0,3,2:T(4,128)S(1)} %copy-done.7, f32[20,8,64,256]{3,0,2,1:T(8,128)S(1)} %fusion.2), kind=kOutput, calls=%fused_computation.66 | convolution fusion | flops 110100480 | bytes 12321088 | tf_op jit(solution)/shard_map/slice | solution.py:162
  850.9 5.8 reshape.129
  856.8 119.4 %copy.118 = f32[2,2,2,8,64,256]{2,5,1,4,0,3:T(8,128)} copy(f32[2,2,2,8,64,256]{5,2,1,0,4,3:T(2,128)} %reshape.129) | data formatting | bytes 8388608 | tf_op jit(solution)/shard_map/reshape | solution.py:152
  976.2 183.6 %reshape.130 = f32[16,128,512]{2,1,0:T(8,128)} reshape(f32[8,2,64,2,256,2]{5,4,3,2,1,0:T(8,128)} %bitcast.74) | data formatting | bytes 8388608 | tf_op jit(solution)/shard_map/reshape | solution.py:155
  1161.0 10.3 fusion.6
  1185.5 9.6 fusion.5
  1197.7 33.7 %copy.121 = f32[2,2,8,64,256]{2,1,4,0,3:T(2,128)} copy(f32[2,2,8,64,256]{4,1,0,3,2:T(2,128)} %reshape.132) | data formatting | bytes 4194304 | tf_op jit(solution)/shard_map/reshape | solution.py:165
  1231.4 20.2 %copy.123 = f32[8,128,512]{2,1,0:T(8,128)} copy(f32[8,128,512]{0,2,1:T(8,128)} %bitcast.232) | data formatting | bytes 4194304
  (68 shorter events, 50.7 us)
Async XLA Ops:
  7.2 182.2 %copy-start = (f32[20,4,32,128]{3,2,1,0:T(8,128)S(1)}, f32[20,4,32,128]{3,2,1,0:T(8,128)}, u32[]{:S(2)}) copy-start(f32[20,4,32,128]{3,2,1,0:T(8,128)} %param.17) | copy-start | bytes 3932164
  7.2 534.3 %all-reduce.4.cloned.1.call-start = ((), (), s32[]{:S(2)}) async-start(), calls=%async_computation | async-start | bytes 32505856 | tf_op jit(solution)/shard_map/psum | solution.py:17
  96.8 89.8 %copy-start.5 = (f32[20,20]{1,0:T(8,128)S(1)}, f32[20,20]{1,0:T(8,128)}, u32[]{:S(2)}) copy-start(f32[20,20]{1,0:T(8,128)} %param.15) | copy-start | bytes 4804
  96.8 90.0 %copy-start.4 = (f32[8,20,20]{2,0,1:T(8,128)S(1)}, f32[8,20,20]{2,0,1:T(8,128)}, u32[]{:S(2)}) copy-start(f32[8,20,20]{2,0,1:T(8,128)} %param.14) | copy-start | bytes 38404
  541.4 6.4 copy-start.6
  734.9 99.8 %copy-start.2 = (f32[20,8,64,256]{3,0,2,1:T(8,128)}, f32[20,8,64,256]{3,0,2,1:T(8,128)S(1)}, u32[]{:S(2)}) copy-start(f32[20,8,64,256]{3,0,2,1:T(8,128)S(1)} %fusion.2) | copy-start | bytes 31457284
  735.0 5.6 copy-start.8
  735.8 424.1 %collective-permute-start.1 = (f32[20,8,1,256]{3,0,2,1:T(8,128)}, f32[20,8,1,256]{3,0,2,1:T(8,128)}, u32[]{:S(2)}, u32[]{:S(2)}) collective-permute-start(f32[20,8,1,256]{3,0,2,1:T(8,128)} %slice.47), channel_id=1, source_target_pairs={{1,0},{0,1},{3,2},{2,3},{5,4},{4,5},{7,6},{6,7},{9,8},{8,9},{11,10... | collective-permute-start | bytes 491528 | tf_op jit(solution)/shard_map/ppermute | solution.py:23
  737.3 11.0 copy-start.12
  737.3 445.2 %collective-permute-start = (f32[20,1,64,256]{3,2,1,0:T(8,128)}, f32[20,1,64,256]{3,2,1,0:T(8,128)}, u32[]{:S(2)}, u32[]{:S(2)}) collective-permute-start(f32[20,1,64,256]{3,2,1,0:T(8,128)} %copy.119), channel_id=1, source_target_pairs={{2,0},{4,2},{6,4},{8,6},{10,8},{12,10},{14,12},{16,14},{18,16},{20... | collective-permute-start | bytes 3932168 | tf_op jit(solution)/shard_map/ppermute | solution.py:23
  748.3 86.5 %copy-start.7 = (f32[4,20,1,1]{1,0,3,2:T(4,128)S(1)}, f32[4,20,1,1]{1,0,3,2:T(4,128)}, u32[]{:S(2)}) copy-start(f32[4,20,1,1]{1,0,3,2:T(4,128)} %constant.107) | copy-start | bytes 964
  976.2 183.6 %copy-start.11 = (f32[4,20,1]{1,0,2:T(4,128)S(1)}, f32[4,20,1]{1,0,2:T(4,128)}, u32[]{:S(2)}) copy-start(f32[4,20,1]{1,0,2:T(4,128)} %constant.111) | copy-start | bytes 964
  976.2 184.8 %copy-start.3 = (f32[4,8,63,256]{3,0,2,1:T(4,128)S(1)}, f32[4,8,63,256]{3,0,2,1:T(4,128)}, u32[]{:S(2)}) copy-start(f32[4,8,63,256]{3,0,2,1:T(4,128)} %fusion.52) | copy-start | bytes 6193156
  976.2 184.8 %copy-start.10 = (f32[4,20,1,1]{1,0,3,2:T(4,128)S(1)}, f32[4,20,1,1]{1,0,3,2:T(4,128)}, u32[]{:S(2)}) copy-start(f32[4,20,1,1]{1,0,3,2:T(4,128)} %constant.109) | copy-start | bytes 964
  1178.6 3.9 copy-start.13
  1178.6 6.9 copy-start.9
  1231.4 20.2 %copy-start.1 = (f32[20,4,32,128]{3,2,1,0:T(8,128)S(1)}, f32[20,4,32,128]{3,2,1,0:T(8,128)}, u32[]{:S(2)}) copy-start(f32[20,4,32,128]{3,2,1,0:T(8,128)} %param.17) | copy-start | bytes 3932164
Sparse Core Ops, SparseCore 0:
  96.9 444.4 all-reduce.3
where the time goes:
time: 1280 us; the launch traced here: 1260 us
  local copies, waits for them, and re-layouts  575 us (45%)
  waiting for transfers between devices  349 us (27%)
  matrix products  195 us (15%)
  blocking collectives  85.6 us (7%)
  other arithmetic  31.6 us (2%)
  between operations  19.1 us (1%)
    psum x1, waiting for transfers between devices, from_root(): return lax.psum(block, axis)  349 us
    reshape x1, local copies, waits for them, and re-layouts, shards(): field_values = values.reshape(2 * fine_planes, 2 * fine_rows, 2 * fine_cols)  184 us
    reshape x2, local copies, waits for them, and re-layouts, shards(): values = expand(inner, fine).reshape(2, 2, 2, fine_planes, fine_rows, fin...  125 us
    reshape x3, local copies, waits for them, and re-layouts, descend(): kids.reshape(2, 2, 2, count, planes, rows_y, cols_x)  93.8 us
    slice x1, matrix products, shards(): south_next = jnp.concatenate([south_faces[:, :, 1:], beside], axis=2)  86.5 us
    psum x1, blocking collectives, from_root(): return lax.psum(block, axis)  85.6 us
    unnamed x32, local copies, waits for them, and re-layouts  51 us
    reshape x3, local copies, waits for them, and re-layouts, descend(): return kids.reshape(count, 2 * planes, 2 * rows_y, 2 * cols_x)  44.1 us
  transfers between devices with their start and end apart: 3, of which 1 were waited for; matrix products, arithmetic and copies ran while one was open for 36% of the time, Pallas kernels for 0%

commit v1 on v0

v1 whole, which is shorter than its diff:
```python
import functools
import math

import jax
import jax.numpy as jnp
import numpy as np
from jax import lax
from jax.experimental import pallas as pl
from jax.experimental.pallas import tpu as pltpu
from jax.sharding import PartitionSpec as P

LEVELS = 8
ROOTS = 2
BANKS = LEVELS - 2
LANES = 128
F32 = jnp.float32
BF16 = jnp.bfloat16
HI = lax.Precision.HIGHEST


def legendre(order, point):
    values = [1.0, point, 1.5 * point * point - 0.5, 2.5 * point * point * point - 1.5 * point]
    return values[order]


def basis_row(point):
    w_coord, v_coord, u_coord = point
    entry = []
    for deg_x in range(4):
        for deg_y in range(4):
            for deg_z in range(4):
                if deg_x + deg_y + deg_z <= 3:
                    factor = math.sqrt((2 * deg_x + 1) * (2 * deg_y + 1) * (2 * deg_z + 1))
                    entry.append(
                        factor
                        * legendre(deg_x, u_coord)
                        * legendre(deg_y, v_coord)
                        * legendre(deg_z, w_coord)
                    )
    return np.array(entry)


def shifted(block, axis, distance):
    devices = range(lax.axis_size(axis))
    route = [((i - distance) % len(devices), i) for i in devices]
    return lax.ppermute(block, axis, route)


def offset_of(level):
    return ROOTS * (8**level - 1) // 7


def round_up(size, unit):
    return -(-size // unit) * unit


class Region:
    def __init__(self, level, n_slab, n_pencil):
        side = 2**level
        self.level = level
        self.nx = ROOTS * side
        self.plane = side * self.nx
        self.whole = self.plane % LANES != 0
        rows = max(1, side // n_pencil)
        self.split = (not self.whole) and (rows * self.nx) % LANES == 0
        self.ny = rows if self.split else side
        self.nz = side if self.whole else max(1, side // n_slab)
        self.count = self.nz * self.ny * self.nx
        self.padded = round_up(self.count, LANES)
        self.n_slab = n_slab
        self.side = side

    def first_plane(self, slab):
        return 0 * slab if self.whole else (slab * self.side) // self.n_slab

    def first_row(self, pencil):
        return pencil * self.ny if self.split else 0 * pencil


def regions_of(n_slab, n_pencil):
    regions = [Region(level, n_slab, n_pencil) for level in range(BANKS)]
    head = [r for r in regions if r.whole]
    tail = [r for r in regions if not r.whole]
    head_width = round_up(offset_of(len(head)), LANES)
    width = head_width
    for r in tail:
        r.start = width
        width += r.count
    return regions, head, tail, head_width, width


def prep_kernel(n_slab, n_pencil, info, bank, out, end):
    regions, head, tail, head_width, width = regions_of(n_slab, n_pencil)
    step = pl.program_id(0)
    pencil = info[0]
    total = bank.shape[2]
    last = total // LANES * LANES
    count = bank.shape[1]

    @pl.when(step == 0)
    def _():
        end[...] = jnp.zeros_like(end)
        if total > last:
            end[:, : total - last] = bank[0, :, last:total]

    lane = lax.broadcasted_iota(jnp.int32, (count, head_width), 1)
    own = jnp.zeros((count, head_width), jnp.int32)
    for r in head:
        own = jnp.where((lane >= offset_of(r.level)), info[1 + r.level], own)
    out[0, :, :head_width] = jnp.where(own > 0, bank[0, :, :head_width], 0.0)
    lanes = lax.broadcasted_iota(jnp.int32, (count, LANES), 1)
    for r in tail:
        shift = offset_of(r.level) % LANES
        owned = info[1 + r.level] > 0
        pieces = r.nz if r.split else 1
        size = r.count // pieces
        for z in range(pieces):
            first = (
                offset_of(r.level) - shift
                + (r.first_plane(step) + z) * r.plane
                + r.first_row(pencil) * r.nx
            )
            chunks = []
            for c in range(size // LANES + 1):
                at = first + c * LANES
                safe = pl.multiple_of(jnp.minimum(at, last - LANES), LANES)
                chunk = bank[0, :, pl.ds(safe, LANES)]
                if c == size // LANES:
                    chunk = jnp.where(at >= last, end[...], chunk)
                chunks.append(pltpu.roll(chunk, (LANES - shift) % LANES, 1))
            for c in range(size // LANES):
                piece = jnp.where(lanes < LANES - shift, chunks[c], chunks[c + 1])
                base = r.start + z * size + c * LANES
                out[0, :, base : base + LANES] = jnp.where(owned, piece, 0.0)


def split2(value):
    high = value.astype(BF16)
    low = (value - high.astype(F32)).astype(BF16)
    return high, low


def dot(left, right):
    return jnp.dot(left, right, preferred_element_type=F32)


def chain_kernel(n_slab, n_pencil, info, received, w_high, w_low, out, noise):
    regions, head, tail, head_width, width = regions_of(n_slab, n_pencil)
    slab, pencil = info[0], info[1]
    count = received.shape[0]
    padded_count = round_up(count, 8)
    noise[...] = jnp.zeros_like(noise)
    noise[:count, :] = received[...]
    parent = None
    for r in regions:
        if r.whole:
            block = noise[:, :head_width]
            start = offset_of(r.level)
            if start:
                block = pltpu.roll(block, head_width - start, 1)
            block = block[:, : r.padded]
        else:
            block = noise[:, r.start : r.start + r.padded]
        if parent is None:
            spread = jnp.zeros((8 * padded_count, r.padded), F32)
        else:
            q = regions[r.level - 1]

            def cells(shape, dim):
                cell = lax.broadcasted_iota(jnp.int32, shape, dim)
                log = lambda n: int(math.log2(n))
                x = cell & (r.nx - 1)
                y = ((cell >> log(r.nx)) & (r.ny - 1)) + r.first_row(pencil)
                z = (cell >> log(r.nx * r.ny)) + r.first_plane(slab)
                return x, y, z

            x, y, z = cells((q.padded, r.padded), 1)
            source = (
                ((z >> 1) - q.first_plane(slab)) * (q.ny * q.nx)
                + ((y >> 1) - q.first_row(pencil)) * q.nx
                + (x >> 1)
            )
            pick = jnp.where(
                lax.broadcasted_iota(jnp.int32, (q.padded, r.padded), 0) == source, 1.0, 0.0
            ).astype(BF16)
            p1, p2 = split2(parent)
            p3 = (parent - p1.astype(F32) - p2.astype(F32)).astype(BF16)
            up = dot(p1, pick) + dot(p2, pick) + dot(p3, pick)
            up = up[:padded_count]
            x, y, z = cells((padded_count, r.padded), 1)
            octant = 4 * (z & 1) + 2 * (y & 1) + (x & 1)
            spread = jnp.concatenate(
                [jnp.where(octant == o, up, 0.0) for o in range(8)], axis=0
            )
        stack = jnp.concatenate([spread, block], axis=0)
        high, low = split2(stack)
        parent = dot(w_high[...], high) + dot(w_high[...], low) + dot(w_low[...], high)
    out[...] = parent


def upsampled(parent, cols):
    lanes = parent.shape[1]
    source = lax.broadcasted_iota(jnp.int32, (lanes, 2 * cols), 0)
    target = lax.broadcasted_iota(jnp.int32, (lanes, 2 * cols), 1)
    wanted = jnp.where(target < cols, 2 * source, 2 * source + 1 + cols)
    pick = jnp.where(wanted == target, 1.0, 0.0).astype(BF16)
    high, low = split2(parent)
    up_high = dot(high, pick).astype(BF16)
    up_low = dot(low, pick).astype(BF16)
    return (up_high[:, :cols], up_high[:, cols:]), (up_low[:, :cols], up_low[:, cols:])


def product(weights, noise, highs, lows):
    noise_high, noise_low = split2(noise)
    high = [noise_high, *highs]
    low = [noise_low, *lows]
    return dot(weights, jnp.concatenate(high + low + high, axis=0))


def middle_kernel(per, info, upper, noise, weights, out):
    count, _, rows, lanes = upper.shape
    cols = noise.shape[3]
    highs, lows = upsampled(upper[:, 0].reshape(count * rows, lanes), cols)
    for i in range(per):
        octz = i if per == 2 else info[0]
        result = product(
            weights[octz], noise[:, i].reshape(count * 2 * rows, cols), highs, lows
        )
        out[:, i] = result.reshape(count, 2 * rows, cols)


def interleave(even, odd):
    rows, cols = even.shape
    lane = lax.broadcasted_iota(jnp.int32, (rows, LANES), 1)
    half = lane >> 1
    first = (lane & 1) == 0
    parts = []
    for j in range(2 * cols // LANES):
        at = (j // 2) * LANES
        index = half + (j % 2) * (LANES // 2)
        a = jnp.take_along_axis(even[:, at : at + LANES], index, axis=1)
        b = jnp.take_along_axis(odd[:, at : at + LANES], index, axis=1)
        parts.append(jnp.where(first, a, b))
    return jnp.concatenate(parts, axis=1)


def fine_kernel(
    middle, noise, weights, field, zface, yface, lower, south, carry_z, carry_y
):
    count, _, rows, lanes = middle.shape
    cols = noise.shape[3]
    tile = 2 * rows
    depth_step, row_step = pl.program_id(0), pl.program_id(1)

    @pl.when(depth_step == 0)
    def _():
        carry_z[row_step] = jnp.zeros(carry_z.shape[1:], F32)

    @pl.when(row_step == 0)
    def _():
        carry_y[...] = jnp.zeros_like(carry_y)

    highs, lows = upsampled(middle[:, 0].reshape(count * rows, lanes), cols)
    above = carry_z[row_step]
    row = lax.broadcasted_iota(jnp.int32, (tile, 2 * cols), 0)
    for octz in (1, 0):
        result = product(
            weights[octz], noise[:, octz].reshape(count * tile, cols), highs, lows
        )
        at = 0

        def pair(size):
            nonlocal at
            even = result[at : at + size]
            odd = result[at + size : at + 2 * size]
            at += 2 * size
            return interleave(even, odd)

        for half in range(2):
            field[2 * octz + half] = pair(2 * tile)
        zface[octz] = pair(2 * tile) + above
        above = pair(2 * tile)
        for half in range(2):
            value = pair(tile)
            edge = carry_y[octz, half : half + 1, :]
            yface[2 * octz + half] = value + jnp.where(row == tile - 1, edge, 0.0)
        edge = pair(8)
        carry_y[octz] = edge
        south[0, octz] = edge
    carry_z[row_step] = above
    lower[...] = above


def fine_rows(tile):
    table, index = [], {}

    def entry(point, scale):
        key = (point, scale)
        if key not in index:
            index[key] = len(table)
            table.append(scale * basis_row(point))
        return index[key]

    halves = [-0.5, 0.5]
    rows = []
    for pz in halves:
        for px in halves:
            for y in range(tile):
                for py in halves:
                    rows.append([(entry((pz, py, px), 1.0), y)])
    for w in (1.0, -1.0):
        for px in halves:
            for y in range(tile):
                for py in halves:
                    rows.append([(entry((w, py, px), 0.5), y)])
    for pz in halves:
        for px in halves:
            for y in range(tile):
                terms = [(entry((pz, 1.0, px), 0.5), y)]
                if y + 1 < tile:
                    terms.append((entry((pz, -1.0, px), 0.5), y + 1))
                rows.append(terms)
    for px in halves:
        for pz in halves:
            rows.append([(entry((pz, -1.0, px), 0.5), 0)])
        rows.extend([[]] * 6)
    return np.array(table), rows


def packed_weights(table, rows, tile, child_maps, innovation):
    count = innovation.shape[0]
    entries = table.shape[0]
    columns = 2 * count * tile
    chan = np.zeros((3 * count, columns), np.float32)
    fine_y = np.zeros((columns,), np.int64)
    is_noise = np.zeros((columns,), bool)
    c = 0
    for block, size in ((0, tile), (1, tile // 2), (2, tile // 2)):
        for k in range(count):
            for y in range(size):
                chan[block * count + k, c] = 1
                fine_y[c] = y
                is_noise[c] = block == 0
                c += 1
    picks, masks = [], []
    for term in range(max(len(r) for r in rows)):
        pick = np.zeros((len(rows), 2 * entries), np.float32)
        mask = np.zeros((len(rows), columns), bool)
        for i, terms in enumerate(rows):
            if term < len(terms):
                q, y = terms[term]
                pick[i, (y % 2) * entries + q] = 1
                mask[i] = np.where(is_noise, fine_y == y, fine_y == y // 2)
        picks.append(pick)
        masks.append(mask)
    table = jnp.asarray(table, F32)
    own = jnp.dot(table, innovation, precision=HI)
    maps = jnp.einsum("qk,okn->oqn", table, child_maps, precision=HI)
    out = []
    for octz in range(2):
        small = jnp.concatenate(
            [
                jnp.concatenate(
                    [own, maps[4 * octz + 2 * octy], maps[4 * octz + 2 * octy + 1]], axis=1
                )
                for octy in range(2)
            ],
            axis=0,
        )
        wide = jnp.dot(small, jnp.asarray(chan), precision=HI)
        total = 0.0
        for pick, mask in zip(picks, masks):
            part = jnp.dot(jnp.asarray(pick), wide, precision=HI)
            total = total + jnp.where(jnp.asarray(mask), part, 0.0)
        out.append(total)
    full = jnp.stack(out)
    high = lax.reduce_precision(full, 8, 7)
    low = full - high
    return jnp.concatenate([high, high, low], axis=2).astype(BF16)


def shards(n_slab, n_pencil, owner_map, window_start, child_maps, innovation, bank,
           noise_middle, noise_finest):
    slab = lax.axis_index("slab").astype(jnp.int32)
    pencil = lax.axis_index("pencil").astype(jnp.int32)
    regions, head, tail, head_width, width = regions_of(n_slab, n_pencil)
    count = innovation.shape[0]
    owners = lax.dynamic_slice(owner_map, (window_start[0],), (BANKS,))
    info = jnp.concatenate([pencil[None], (owners == slab).astype(jnp.int32)])
    smem = pl.BlockSpec(memory_space=pltpu.SMEM)
    windows = pl.pallas_call(
        functools.partial(prep_kernel, n_slab, n_pencil),
        grid=(n_slab,),
        in_specs=[smem, pl.BlockSpec(bank.shape, lambda s: (0, 0, 0))],
        out_specs=pl.BlockSpec((1, count, width), lambda s: (s, 0, 0)),
        out_shape=jax.ShapeDtypeStruct((n_slab, count, width), F32),
        scratch_shapes=[pltpu.VMEM((count, LANES), F32)],
        name="windows",
    )(info, bank)
    received = lax.psum_scatter(windows, "slab", scatter_dimension=0, tiled=True)[0]

    padded = round_up(count, 8)
    wide = round_up(padded, 16)
    maps = jnp.pad(child_maps, ((0, 0), (0, wide - count), (0, padded - count)))
    flat = jnp.concatenate(
        [maps[o] for o in range(8)]
        + [jnp.pad(innovation, ((0, wide - count), (0, wide - count)))],
        axis=1,
    )
    flat_high = lax.reduce_precision(flat, 8, 7)
    place = jnp.stack([slab, pencil])
    vmem = pl.BlockSpec(memory_space=pltpu.VMEM)
    top = regions[-1]
    upper = pl.pallas_call(
        functools.partial(chain_kernel, n_slab, n_pencil),
        in_specs=[smem, vmem, vmem, vmem],
        out_specs=vmem,
        out_shape=jax.ShapeDtypeStruct((wide, top.padded), F32),
        scratch_shapes=[pltpu.VMEM((wide, width), F32)],
        name="coarse",
    )(place, received, flat_high.astype(BF16), (flat - flat_high).astype(BF16))
    upper = upper[:count].reshape(count, top.nz, top.ny, top.nx)

    tile = 16
    half = tile // 2
    eye_rows = [[(k, y)] for k in range(count) for y in range(tile)]
    middle_weights = packed_weights(np.eye(count), eye_rows, tile, child_maps, innovation)
    _, planes, rows, cols = noise_middle.shape
    per = planes // top.nz
    octz = (slab * planes) % 2
    middle = pl.pallas_call(
        functools.partial(middle_kernel, per),
        grid=(top.nz, rows // tile),
        in_specs=[
            smem,
            pl.BlockSpec((count, 1, half, top.nx), lambda z, y: (0, z, y, 0)),
            pl.BlockSpec((count, per, tile, cols), lambda z, y: (0, z, y, 0)),
            vmem,
        ],
        out_specs=pl.BlockSpec((count, per, tile, cols), lambda z, y: (0, z, y, 0)),
        out_shape=jax.ShapeDtypeStruct(noise_middle.shape, F32),
        name="middle",
    )(octz[None], upper, noise_middle, middle_weights)

    table, row_list = fine_rows(tile)
    fine_weights = packed_weights(table, row_list, tile, child_maps, innovation)
    _, fine_planes, fine_y, fine_x = noise_finest.shape
    nz, ny = planes, fine_y // tile
    out_x = 2 * fine_x

    def block(*where):
        def index(z, y):
            at = {"z": nz - 1 - z, "y": ny - 1 - y}
            return tuple(at.get(w, 0) for w in where)

        return index

    field, zface, yface, lower, south = pl.pallas_call(
        fine_kernel,
        grid=(nz, ny),
        in_specs=[
            pl.BlockSpec((count, 1, half, cols), block(0, "z", "y", 0)),
            pl.BlockSpec((count, 2, tile, fine_x), block(0, "z", "y", 0)),
            vmem,
        ],
        out_specs=[
            pl.BlockSpec((4, 2 * tile, out_x), block("z", "y", 0)),
            pl.BlockSpec((2, 2 * tile, out_x), block("z", "y", 0)),
            pl.BlockSpec((4, tile, out_x), block("z", "y", 0)),
            pl.BlockSpec((2 * tile, out_x), block("y", 0)),
            pl.BlockSpec((1, 2, 8, out_x), block("z", 0, 0, 0)),
        ],
        out_shape=[
            jax.ShapeDtypeStruct((2 * fine_planes, 2 * fine_y, out_x), F32),
            jax.ShapeDtypeStruct((fine_planes, 2 * fine_y, out_x), F32),
            jax.ShapeDtypeStruct((2 * fine_planes, fine_y, out_x), F32),
            jax.ShapeDtypeStruct((2 * fine_y, out_x), F32),
            jax.ShapeDtypeStruct((nz, 2, 8, out_x), F32),
        ],
        scratch_shapes=[
            pltpu.VMEM((ny, 2 * tile, out_x), F32),
            pltpu.VMEM((2, 8, out_x), F32),
        ],
        name="fine",
    )(middle, noise_finest, fine_weights)
    above = shifted(lower, "slab", -1)
    beside = shifted(south[:, :, :2].reshape(2 * fine_planes, out_x), "pencil", -1)
    zface = zface.at[-1].add(above)
    yface = yface.at[:, -1].add(beside)
    return field, zface, yface


def solution(mesh):
    placed = (
        P(),
        P(),
        P(),
        P(),
        P("slab", None, None),
        P(None, "slab", "pencil", None),
        P(None, "slab", "pencil", None),
    )
    return jax.shard_map(
        functools.partial(shards, mesh.shape["slab"], mesh.shape["pencil"]),
        mesh=mesh,
        in_specs=placed,
        out_specs=(P("slab", "pencil", None), P("slab", "pencil", None), P("slab", "pencil", None)),
        check_vma=False,
    )
```

time: 1280 us -> 227 us (0.18); the launches traced: 1260 us -> 227 us
  local copies, waits for them, and re-layouts: 575 us -> 11.7 us
  waiting for transfers between devices: 349 us -> 130 us
  matrix products: 195 us -> 7.01 us
  blocking collectives: 85.6 us -> 0 us
  Pallas kernels: 0 us -> 51 us
  other arithmetic: 31.6 us -> 8.52 us
    reshape x13 -> x2, local copies, waits for them, and re-layouts: 490 us -> 0.88 us  [the longest x1 0.86 us: shards(): upper = upper[:count].reshape(count, top.nz, top.ny, top.nx)]
    psum x1 -> x0, waiting for transfers between devices: 349 us -> none  [from_root(): return lax.psum(block, axis)]
    unnamed x1 -> x2, waiting for transfers between devices: 0.02 us -> 127 us
    slice x2 -> x0, matrix products: 103 us -> none  [the longest x1 86.5 us: shards(): south_next = jnp.concatenate([south_faces[:, :, 1:], beside], axis=2)]
    psum x1 -> x0, blocking collectives: 85.6 us -> none  [from_root(): return lax.psum(block, axis)]
    dot_general x20 -> x14, matrix products: 92 us -> 7.01 us  [the longest x6 5.02 us: packed_weights(): part = jnp.dot(jnp.asarray(pick), wide, precision=HI)]
    pallas_call x0 -> x4, Pallas kernels: none -> 51 us  [the longest x1 29.5 us: shards(): pl.pallas_call(fine_kernel, grid=(nz, ny), in_specs=[pl.BlockSpec((count,...]
    unnamed x32 -> x30, local copies, waits for them, and re-layouts: 51 us -> 7.09 us
  transfers between devices with their start and end apart: 3 -> 3, of which waited for: 1 -> 2; matrix products, arithmetic and copies ran while one was open for 36% -> 7% of each run, Pallas kernels for 0% -> 0%
where the time goes in v1:
time: 227 us
  waiting for transfers between devices  130 us (57%)
  Pallas kernels  51 us (22%)
  between operations  15 us (7%)
  local copies, waits for them, and re-layouts  11.7 us (5%)
  other arithmetic  8.52 us (4%)
  matrix products  7.01 us (3%)
  starting transfers between devices  3.2 us (1%)
    unnamed x2, waiting for transfers between devices  127 us
    pallas_call x1, Pallas kernels, shards(): pl.pallas_call(fine_kernel, grid=(nz, ny), in_specs=[pl.BlockSpec((count,...  29.5 us
    pallas_call x1, Pallas kernels, shards(): pl.pallas_call(functools.partial(prep_kernel, n_slab, n_pencil), grid=(n_...  10.1 us
    unnamed x30, local copies, waits for them, and re-layouts  7.09 us
    pallas_call x1, Pallas kernels, shards(): pl.pallas_call(functools.partial(middle_kernel, per), grid=(top.nz, rows...  6.68 us
    dot_general x6, matrix products, packed_weights(): part = jnp.dot(jnp.asarray(pick), wide, precision=HI)  5.02 us
    pallas_call x1, Pallas kernels, shards(): pl.pallas_call(functools.partial(chain_kernel, n_slab, n_pencil), in_spec...  4.69 us
  transfers between devices with their start and end apart: 3, of which 2 were waited for; matrix products, arithmetic and copies ran while one was open for 7% of the time, Pallas kernels for 0%

profile of v1, /device:TPU:0, one launch (start us, length us, event | category | flops | bytes accessed | tf_op | source)
XLA Modules:
  0.0 226.9 jit_solution(6173626141758480956)
XLA Ops:
  7.9 6.2 %copy.24.bank = f32[1,20,74898]{2,1,0:T(8,128)} copy(f32[1,20,74898]{2,0,1:T(1,128)} %param.25) | data formatting | bytes 11983680 | tf_op args[4]
  14.8 10.1 %windows.1 = f32[16,20,2688]{2,1,0:T(8,128)} custom-call(s32[7]{0:T(128)} %pad_add_fusion.1.info, f32[1,20,74898]{2,1,0:T(8,128)} %copy.24.bank), custom_call_target="tpu_custom_call" | custom-call | tf_op jit(solution)/shard_map/windows/pallas_call | solution.py:391
  25.0 0.8 copy-done.1
  26.0 0.7 pad_add_fusion.info
  27.4 0.8 fusion.6
  28.6 0.8 fusion.7
  30.4 0.8 convolution_select_fusion.1
  31.3 0.9 fusion.3
  32.5 0.8 convolution_select_fusion.3
  33.3 0.9 fusion.5
  35.1 1.6 pad_maximum_fusion.1.weights
  36.8 1.7 pad_maximum_fusion.weights
  38.4 126.7 %reduce-scatter.4.cloned.1.call-done = f32[1,20,2688]{2,1,0:T(8,128)} async-done(((f32[16,20,2688]{2,1,0:T(8,128)}), f32[1,20,2688]{2,1,0:T(8,128)}) %reduce-scatter.4.cloned.1.call-update) | async-done | bytes 215056
  165.1 4.7 %coarse.1 = f32[32,2048]{1,0:T(8,128)} custom-call(s32[2]{0:T(128)} %pad_add_fusion.info, f32[20,2688]{1,0:T(8,128)} %bitcast.97, bf16[32,224]{1,0:T(8,128)(2,1)} %get-tuple-element.66.w_high, bf16[32,224]{1,0:T(8,128)(2,1)} %get-tuple-element.65.w_low), custom_call_target="tpu_custom_call" | custom-call | tf_op jit(solution)/shard_map/coarse/pallas_call | solution.py:414
  169.8 0.9 slice.150
  170.7 0.9 reshape.73.upper
  171.6 6.7 %middle.1 = f32[20,4,32,128]{3,2,1,0:T(8,128)} custom-call(s32[1]{0:T(128)} %bitcast.info, f32[20,2,16,64]{3,2,1,0:T(8,128)} %reshape.73.upper, f32[20,4,32,128]{3,2,1,0:T(8,128)} %noise.2, bf16[2,320,1920]{2,1,0:T(8,128)(2,1)} %pad_maximum_fusion.1.weights), custom_call_target="tpu_custom_call" | custom-call | tf_op jit(solution)/shard_map/middle/pallas_call | solution.py:431
  178.3 29.5 %fine.1 = (f32[16,128,512]{2,1,0:T(8,128)}, f32[8,128,512]{2,1,0:T(8,128)}, f32[16,64,512]{2,1,0:T(8,128)}, f32[128,512]{1,0:T(8,128)}, f32[4,2,8,512]{3,2,1,0:T(8,128)}) custom-call(f32[20,4,32,128]{3,2,1,0:T(8,128)} %middle.1, f32[20,8,64,256]{3,2,1,0:T(8,128)} %noise.3, bf16[2,336,1920]{2,1,0:T(8,128)(2,1)} %pad_maximum_fusion.weights), custom_call_target="tpu_custom_call" | custom-call | tf_op jit(solution)/shard_map/fine/pallas_call | solution.py:458
  207.8 0.9 slice.149
  208.8 3.1 %collective-permute-start = (f32[128,512]{1,0:T(8,128)}, f32[128,512]{1,0:T(8,128)S(1)}, u32[]{:S(2)}, u32[]{:S(2)}) collective-permute-start(f32[128,512]{1,0:T(8,128)} %get-tuple-element.34), channel_id=1, source_target_pairs={{2,0},{4,2},{6,4},{8,6},{10,8},{12,10},{14,12},{16,14},{18,16},{20... | collective-permute-start | bytes 786440 | tf_op jit(solution)/shard_map/ppermute | solution.py:46
  211.9 1.0 reshape_add_fusion
  212.9 1.8 scatter-add.9
  214.7 3.7 %collective-permute-done = f32[128,512]{1,0:T(8,128)S(1)} collective-permute-done((f32[128,512]{1,0:T(8,128)}, f32[128,512]{1,0:T(8,128)S(1)}, u32[]{:S(2)}, u32[]{:S(2)}) %collective-permute-start) | collective-permute-done | bytes 262176 | tf_op jit(solution)/shard_map/ppermute | solution.py:46
  218.4 1.7 fusion.8
  (51 shorter events, 4.3 us)
Async XLA Ops:
  7.2 158.0 %reduce-scatter.4.cloned.1.call-start = ((), (), s32[]{:S(2)}) async-start(), calls=%async_computation.1 | async-start | bytes 4386816
  7.9 6.2 %copy-start.13 = (s32[16]{0:T(128)S(1)}, s32[16]{0:T(128)}, u32[]{:S(2)}) copy-start(s32[16]{0:T(128)} %param.21) | copy-start | bytes 196
  24.9 0.9 copy-start.1
  24.9 0.9 copy-start.8
  24.9 1.7 copy-start.12
  24.9 1.9 copy-start.10
  24.9 2.1 copy-start
  24.9 2.4 %copy-start.4 = (pred[320,640]{1,0:T(32,128)(4,1)S(1)}, pred[320,640]{1,0:T(32,128)(4,1)}, u32[]{:S(2)}) copy-start(pred[320,640]{1,0:T(32,128)(4,1)} %constant.106.clone) | copy-start | bytes 614404
  24.9 2.4 %copy-start.7 = (f32[320,40]{1,0:T(8,128)S(1)}, f32[320,40]{1,0:T(8,128)}, u32[]{:S(2)}) copy-start(f32[320,40]{1,0:T(8,128)} %constant.105.clone) | copy-start | bytes 153604
  28.2 1.5 copy-start.11
  28.2 1.6 copy-start.9
  28.5 1.9 copy-start.3
  28.6 1.9 copy-start.6
  29.4 1.9 copy-start.2
  29.4 1.9 copy-start.5
  208.7 3.2 %collective-permute-start.1 = (f32[16,512]{1,0:T(8,128)S(1)}, f32[16,512]{1,0:T(8,128)S(1)}, u32[]{:S(2)}, u32[]{:S(2)}) collective-permute-start(f32[16,512]{1,0:T(8,128)S(1)} %reshape.75), channel_id=1, source_target_pairs={{1,0},{0,1},{3,2},{2,3},{5,4},{4,5},{7,6},{6,7},{9,8},{8,9},{11,10... | collective-permute-start | bytes 98312 | tf_op jit(solution)/shard_map/ppermute | solution.py:46
  208.8 9.6 %collective-permute-start = (f32[128,512]{1,0:T(8,128)}, f32[128,512]{1,0:T(8,128)S(1)}, u32[]{:S(2)}, u32[]{:S(2)}) collective-permute-start(f32[128,512]{1,0:T(8,128)} %get-tuple-element.34), channel_id=1, source_target_pairs={{2,0},{4,2},{6,4},{8,6},{10,8},{12,10},{14,12},{16,14},{18,16},{20... | collective-permute-start | bytes 786440 | tf_op jit(solution)/shard_map/ppermute | solution.py:46
Sparse Core Ops, SparseCore 0:
  25.1 139.9 reduce-scatter.3

commit v2 on v1

--- a/solution.py
+++ b/solution.py
@@ -388,16 +388,28 @@
     owners = lax.dynamic_slice(owner_map, (window_start[0],), (BANKS,))
     info = jnp.concatenate([pencil[None], (owners == slab).astype(jnp.int32)])
     smem = pl.BlockSpec(memory_space=pltpu.SMEM)
+    inner = 1
+    while inner * inner < n_slab:
+        inner *= 2
+    outer = n_slab // inner
     windows = pl.pallas_call(
         functools.partial(prep_kernel, n_slab, n_pencil),
         grid=(n_slab,),
         in_specs=[smem, pl.BlockSpec(bank.shape, lambda s: (0, 0, 0))],
-        out_specs=pl.BlockSpec((1, count, width), lambda s: (s, 0, 0)),
+        out_specs=pl.BlockSpec(
+            (1, count, width), lambda s: ((s % inner) * outer + s // inner, 0, 0)
+        ),
         out_shape=jax.ShapeDtypeStruct((n_slab, count, width), F32),
         scratch_shapes=[pltpu.VMEM((count, LANES), F32)],
         name="windows",
     )(info, bank)
-    received = lax.psum_scatter(windows, "slab", scatter_dimension=0, tiled=True)[0]
+    near = [[o * inner + i for i in range(inner)] for o in range(outer)]
+    far = [[o * inner + i for o in range(outer)] for i in range(inner)]
+    parts = windows.reshape(inner, outer, count, width)
+    parts = lax.all_to_all(parts, "slab", 0, 0, axis_index_groups=near, tiled=True)
+    parts = jnp.sum(parts, axis=0)
+    parts = lax.all_to_all(parts, "slab", 0, 0, axis_index_groups=far, tiled=True)
+    received = jnp.sum(parts, axis=0)
 
     padded = round_up(count, 8)
     wide = round_up(padded, 16)

time: 227 us -> 158 us (0.70)
  waiting for transfers between devices: 130 us -> 41.5 us
  between operations: 15 us -> 1.59 us
  starting transfers between devices: 3.2 us -> 13 us
  local copies, waits for them, and re-layouts: 11.7 us -> 21.3 us
  matrix products: 7.01 us -> 16.1 us
  other arithmetic: 8.52 us -> 12.2 us
    unnamed x2 -> x0, waiting for transfers between devices: 127 us -> none
    all_to_all x0 -> x2, waiting for transfers between devices: none -> 37.7 us  [the longest x1 19.7 us: shards(): lax.all_to_all(parts, 'slab', 0, 0, axis_index_groups=near, tiled=True)]
    all_to_all x0 -> x2, starting transfers between devices: none -> 10.6 us  [the longest x1 5.32 us: shards(): lax.all_to_all(parts, 'slab', 0, 0, axis_index_groups=near, tiled=True)]
    dot_general x6, matrix products: 5.02 us -> 10.7 us  [packed_weights(): part = jnp.dot(jnp.asarray(pick), wide, precision=HI)]
    reshape x0 -> x1, local copies, waits for them, and re-layouts: none -> 4.78 us  [shards(): parts = windows.reshape(inner, outer, count, width)]
    reduce_sum x0 -> x2, other arithmetic: none -> 2.63 us  [the longest x1 1.87 us: shards(): parts = jnp.sum(parts, axis=0)]
    reduce_sum x0 -> x1, local copies, waits for them, and re-layouts: none -> 2.27 us  [shards(): parts = jnp.sum(parts, axis=0)]
    unnamed x30 -> x40, local copies, waits for them, and re-layouts: 7.09 us -> 6.93 us
  transfers between devices with their start and end apart: 3 -> 4, of which waited for: 2 -> 3; matrix products, arithmetic and copies ran while one was open for 7% -> 18% of each run, Pallas kernels for 0% -> 0%
where the time goes in v2:
time: 158 us; the launch traced here: 157 us
  Pallas kernels  51 us (32%)
  waiting for transfers between devices  41.5 us (26%)
  local copies, waits for them, and re-layouts  21.3 us (13%)
  matrix products  16.1 us (10%)
  starting transfers between devices  13 us (8%)
  other arithmetic  12.2 us (8%)
  between operations  1.59 us (1%)
    pallas_call x1, Pallas kernels, shards(): pl.pallas_call(fine_kernel, grid=(nz, ny), in_specs=[pl.BlockSpec((count,...  29.5 us
    all_to_all x1, waiting for transfers between devices, shards(): lax.all_to_all(parts, 'slab', 0, 0, axis_index_groups=near, tiled=True)  19.7 us
    all_to_all x1, waiting for transfers between devices, shards(): lax.all_to_all(parts, 'slab', 0, 0, axis_index_groups=far, tiled=True)  18 us
    dot_general x6, matrix products, packed_weights(): part = jnp.dot(jnp.asarray(pick), wide, precision=HI)  10.7 us
    pallas_call x1, Pallas kernels, shards(): pl.pallas_call(functools.partial(prep_kernel, n_slab, n_pencil), grid=(n_...  10.1 us
    unnamed x40, local copies, waits for them, and re-layouts  6.93 us
    pallas_call x1, Pallas kernels, shards(): pl.pallas_call(functools.partial(middle_kernel, per), grid=(top.nz, rows...  6.67 us
    all_to_all x1, starting transfers between devices, shards(): lax.all_to_all(parts, 'slab', 0, 0, axis_index_groups=near, tiled=True)  5.32 us
  transfers between devices with their start and end apart: 4, of which 3 were waited for; matrix products, arithmetic and copies ran while one was open for 18% of the time, Pallas kernels for 0%

profile of v2, /device:TPU:0, one launch (start us, length us, event | category | flops | bytes accessed | tf_op | source)
XLA Modules:
  0.0 156.8 jit_solution(16908580596591653187)
XLA Ops:
  1.3 6.2 %copy.34.bank = f32[1,20,74898]{2,1,0:T(8,128)} copy(f32[1,20,74898]{2,0,1:T(1,128)} %param.25) | data formatting | bytes 11983680 | tf_op args[4]
  8.1 10.1 %windows.1 = f32[16,20,2688]{2,1,0:T(8,128)} custom-call(s32[7]{0:T(128)} %pad_add_fusion.1.info, f32[1,20,74898]{2,1,0:T(8,128)} %copy.34.bank), custom_call_target="tpu_custom_call" | custom-call | tf_op jit(solution)/shard_map/windows/pallas_call | solution.py:395
  18.3 4.8 %copy.35 = f32[4,4,20,2688]{3,1,2,0:T(4,128)} copy(f32[4,4,20,2688]{3,2,1,0:T(8,128)} %bitcast.96) | data formatting | bytes 6881280 | tf_op jit(solution)/shard_map/reshape | solution.py:408
  23.1 5.3 %all-to-all-start = ((f32[4,4,20,2688]{3,1,2,0:T(4,128)}), f32[4,4,20,2688]{3,1,2,0:T(4,128)S(1)}, u32[]{:S(2)}, u32[]{:S(2)}) async-start(f32[4,4,20,2688]{3,1,2,0:T(4,128)} %copy.35), calls=%async_computation | async-start | bytes 6881280 | tf_op jit(solution)/shard_map/all_to_all | solution.py:409
  29.9 1.5 fusion.64
  35.0 2.8 %fusion.6 = f32[1,320,640]{2,1,0:T(8,128)} fusion(pred[320,640]{1,0:T(32,128)(4,1)} %constant.106.clone, f32[320,40]{1,0:T(8,128)} %constant.105.clone, f32[40,640]{1,0:T(8,128)S(1)} %fusion.36), kind=kOutput, calls=%fused_computation.19 | convolution fusion | flops 98508800 | bytes 1177600 | tf_op jit(solution)/shard_map/dot_general | solution.py:373
  39.1 2.7 %fusion.7 = f32[1,320,640]{2,1,0:T(8,128)} fusion(pred[320,640]{1,0:T(32,128)(4,1)} %constant.106.clone, f32[320,40]{1,0:T(8,128)} %constant.105.clone, f32[40,640]{1,0:T(8,128)S(1)} %fusion.32), kind=kOutput, calls=%fused_computation.21 | convolution fusion | flops 98508800 | bytes 1177600 | tf_op jit(solution)/shard_map/dot_general | solution.py:373
  43.5 1.8 %fusion.3 = f32[1,336,640]{2,1,0:T(8,128)} fusion(f32[336,640]{1,0:T(8,128)S(1)} %convolution_select_fusion.1, pred[336,640]{1,0:T(8,128)(4,1)S(1)} %copy-done.7, f32[336,48]{1,0:T(8,128)S(1)} %copy-done.10, f32[48,640]{1,0:T(8,128)S(1)} %fusion.16), kind=kOutput, calls=%fused_computation.12 | convolution fusion | flops 124293120 | bytes 2122752 | tf_op jit(solution)/shard_map/dot_general | solution.py:373
  46.3 1.7 %convolution_select_fusion.3 = f32[336,640]{1,0:T(8,128)} fusion(pred[336,640]{1,0:T(8,128)(4,1)S(1)} %copy-done.9, f32[336,48]{1,0:T(8,128)S(1)} %copy-done.12, f32[48,640]{1,0:T(8,128)S(1)} %fusion.12), kind=kOutput, calls=%fused_computation.17 | convolution fusion | flops 124078080 | bytes 1262592 | tf_op jit(solution)/shard_map/dot_general | solution.py:373
  48.0 19.7 %all-to-all-done = f32[4,4,20,2688]{3,1,2,0:T(4,128)S(1)} async-done(((f32[4,4,20,2688]{3,1,2,0:T(4,128)}), f32[4,4,20,2688]{3,1,2,0:T(4,128)S(1)}, u32[]{:S(2)}, u32[]{:S(2)}) %all-to-all-start) | async-done | bytes 3440672 | tf_op jit(solution)/shard_map/all_to_all | solution.py:409
  67.7 1.9 %reduce_sum.18 = f32[4,20,2688]{2,0,1:T(4,128)} reduce(f32[4,4,20,2688]{3,1,2,0:T(4,128)S(1)} %all-to-all-done, f32[]{:T(128)} %constant.100.clone.1), dimensions={0}, to_apply=%region_0.0 | reduce | flops 645120 | bytes 4300804 | tf_op jit(solution)/shard_map/reduce_sum | solution.py:410
  69.5 2.3 %copy.36 = f32[4,20,2688]{2,1,0:T(8,128)} copy(f32[4,20,2688]{2,0,1:T(4,128)} %reduce_sum.18) | data formatting | bytes 1720320 | tf_op jit(solution)/shard_map/reduce_sum | solution.py:410
  71.8 5.3 %all-to-all-start.1 = ((f32[4,20,2688]{2,1,0:T(8,128)}), f32[4,20,2688]{2,1,0:T(8,128)S(1)}, u32[]{:S(2)}, u32[]{:S(2)}) async-start(f32[4,20,2688]{2,1,0:T(8,128)} %copy.36), calls=%async_computation.1 | async-start | bytes 2064384 | tf_op jit(solution)/shard_map/all_to_all | solution.py:411
  77.1 1.5 reduce-precision_convert_fusion.1
  80.4 1.6 %pad_maximum_fusion.1.weights = bf16[2,320,1920]{2,1,0:T(8,128)(2,1)} fusion(bf16[2,320,640]{2,1,0:T(8,128)(2,1)S(1)} %get-tuple-element.40, bf16[2,320,640]{2,1,0:T(8,128)(2,1)S(1)} %get-tuple-element.39), kind=kLoop, calls=%fused_computation.3 | loop fusion | flops 7372800 | bytes 4096000 | tf_op jit(solution)/shard_map/concatenate | solution.py:379
  82.0 1.7 %pad_maximum_fusion.weights = bf16[2,336,1920]{2,1,0:T(8,128)(2,1)} fusion(bf16[2,336,640]{2,1,0:T(8,128)(2,1)S(1)} %get-tuple-element.38, bf16[2,336,640]{2,1,0:T(8,128)(2,1)S(1)} %get-tuple-element.37), kind=kLoop, calls=%fused_computation | loop fusion | flops 7741440 | bytes 4300800 | tf_op jit(solution)/shard_map/concatenate | solution.py:379
  83.7 18.0 %all-to-all-done.1 = f32[4,20,2688]{2,1,0:T(8,128)S(1)} async-done(((f32[4,20,2688]{2,1,0:T(8,128)}), f32[4,20,2688]{2,1,0:T(8,128)S(1)}, u32[]{:S(2)}, u32[]{:S(2)}) %all-to-all-start.1) | async-done | bytes 860192 | tf_op jit(solution)/shard_map/all_to_all | solution.py:411
  102.5 4.7 %coarse.1 = f32[32,2048]{1,0:T(8,128)} custom-call(s32[2]{0:T(128)} %pad_add_fusion.info, f32[20,2688]{1,0:T(8,128)} %reduce_sum.19.received, bf16[32,224]{1,0:T(8,128)(2,1)} %get-tuple-element.66.w_high, bf16[32,224]{1,0:T(8,128)(2,1)} %get-tuple-element.65.w_low), custom_call_target="tpu_custom_call" | custom-call | tf_op jit(solution)/shard_map/coarse/pallas_call | solution.py:426
  108.9 6.7 %middle.1 = f32[20,4,32,128]{3,2,1,0:T(8,128)} custom-call(s32[1]{0:T(128)} %bitcast.info, f32[20,2,16,64]{3,2,1,0:T(8,128)} %reshape.77.upper, f32[20,4,32,128]{3,2,1,0:T(8,128)} %noise.2, bf16[2,320,1920]{2,1,0:T(8,128)(2,1)} %pad_maximum_fusion.1.weights), custom_call_target="tpu_custom_call" | custom-call | tf_op jit(solution)/shard_map/middle/pallas_call | solution.py:443
  115.6 29.5 %fine.1 = (f32[16,128,512]{2,1,0:T(8,128)}, f32[8,128,512]{2,1,0:T(8,128)}, f32[16,64,512]{2,1,0:T(8,128)}, f32[128,512]{1,0:T(8,128)}, f32[4,2,8,512]{3,2,1,0:T(8,128)}) custom-call(f32[20,4,32,128]{3,2,1,0:T(8,128)} %middle.1, f32[20,8,64,256]{3,2,1,0:T(8,128)} %noise.3, bf16[2,336,1920]{2,1,0:T(8,128)(2,1)} %pad_maximum_fusion.weights), custom_call_target="tpu_custom_call" | custom-call | tf_op jit(solution)/shard_map/fine/pallas_call | solution.py:470
  146.2 2.3 %collective-permute-start = (f32[128,512]{1,0:T(8,128)}, f32[128,512]{1,0:T(8,128)S(1)}, u32[]{:S(2)}, u32[]{:S(2)}) collective-permute-start(f32[128,512]{1,0:T(8,128)} %get-tuple-element.34), channel_id=1, source_target_pairs={{2,0},{4,2},{6,4},{8,6},{10,8},{12,10},{14,12},{16,14},{18,16},{20... | collective-permute-start | bytes 786440 | tf_op jit(solution)/shard_map/ppermute | solution.py:46
  149.5 1.8 %scatter-add.9 = f32[16,64,512]{2,1,0:T(8,128)} dynamic-update-slice(f32[16,64,512]{2,1,0:T(8,128)} %get-tuple-element.35, f32[16,1,512]{2,1,0:T(1,128)S(1)} %reshape_add_fusion, s32[]{:T(128)} %constant.96.clone.1, s32[]{:T(128)} %constant.102.clone.1, s32[]{:T(128)} %constant.96.clone.1) | dynamic-update-slice | bytes 65540 | tf_op jit(solution)/shard_map/scatter-add | solution.py:501
  151.3 3.8 %collective-permute-done = f32[128,512]{1,0:T(8,128)S(1)} collective-permute-done((f32[128,512]{1,0:T(8,128)}, f32[128,512]{1,0:T(8,128)S(1)}, u32[]{:S(2)}, u32[]{:S(2)}) %collective-permute-start) | collective-permute-done | bytes 262176 | tf_op jit(solution)/shard_map/ppermute | solution.py:46
  155.1 1.7 %fusion.8 = f32[8,128,512]{2,1,0:T(8,128)} fusion(f32[8,128,512]{2,1,0:T(8,128)} %get-tuple-element.33, f32[128,512]{1,0:T(8,128)S(1)} %collective-permute-done), kind=kLoop, calls=%fused_computation.25 | loop fusion | flops 65536 | bytes 786432 | tf_op jit(solution)/shard_map/scatter-add | solution.py:500
  (66 shorter events, 16.0 us)
Async XLA Ops:
  1.3 6.2 %copy-start.18 = (s32[16]{0:T(128)S(1)}, s32[16]{0:T(128)}, u32[]{:S(2)}) copy-start(s32[16]{0:T(128)} %param.21) | copy-start | bytes 196
  23.1 5.3 %copy-start.6 = (f32[8,20,20]{2,0,1:T(8,128)S(1)}, f32[8,20,20]{2,0,1:T(8,128)}, u32[]{:S(2)}) copy-start(f32[8,20,20]{2,0,1:T(8,128)} %param.23) | copy-start | bytes 38404
  23.1 6.0 %copy-start.16 = (f32[20,20,1]{1,0,2:T(8,128)S(1)}, f32[20,20,1]{1,0,2:T(8,128)}, u32[]{:S(2)}) copy-start(f32[20,20,1]{1,0,2:T(8,128)} %constant.119) | copy-start | bytes 4804
  23.1 6.9 %copy-start.13 = (f32[20,20]{1,0:T(8,128)S(1)}, f32[20,20]{1,0:T(8,128)}, u32[]{:S(2)}) copy-start(f32[20,20]{1,0:T(8,128)} %param.24) | copy-start | bytes 4804
  23.1 44.6 %all-to-all-start = ((f32[4,4,20,2688]{3,1,2,0:T(4,128)}), f32[4,4,20,2688]{3,1,2,0:T(4,128)S(1)}, u32[]{:S(2)}, u32[]{:S(2)}) async-start(f32[4,4,20,2688]{3,1,2,0:T(4,128)} %copy.35), calls=%async_computation | async-start | bytes 6881280 | tf_op jit(solution)/shard_map/all_to_all | solution.py:409
  33.5 8.3 %copy-start.14 = (f32[20,20]{1,0:T(8,128)S(1)}, f32[20,20]{1,0:T(8,128)}, u32[]{:S(2)}) copy-start(f32[20,20]{1,0:T(8,128)} %param.24) | copy-start | bytes 4804
  33.6 8.3 %copy-start.17 = (f32[24,20]{1,0:T(8,128)S(1)}, f32[24,20]{1,0:T(8,128)}, u32[]{:S(2)}) copy-start(f32[24,20]{1,0:T(8,128)} %constant.107.clone) | copy-start | bytes 5764
  33.6 8.4 %copy-start.15 = (f32[24,20,1]{1,0,2:T(8,128)S(1)}, f32[24,20,1]{1,0,2:T(8,128)}, u32[]{:S(2)}) copy-start(f32[24,20,1]{1,0,2:T(8,128)} %constant.120) | copy-start | bytes 5764
  33.6 8.7 %copy-start.3 = (f32[60,640]{1,0:T(8,128)S(1)}, f32[60,640]{1,0:T(8,128)}, u32[]{:S(2)}) copy-start(f32[60,640]{1,0:T(8,128)} %constant.104.clone) | copy-start | bytes 460804
  33.6 9.0 %copy-start.9 = (pred[336,640]{1,0:T(8,128)(4,1)S(1)}, pred[336,640]{1,0:T(8,128)(4,1)}, u32[]{:S(2)}) copy-start(pred[336,640]{1,0:T(8,128)(4,1)} %constant.109.clone) | copy-start | bytes 645124
  33.6 9.0 %copy-start.12 = (f32[336,48]{1,0:T(8,128)S(1)}, f32[336,48]{1,0:T(8,128)}, u32[]{:S(2)}) copy-start(f32[336,48]{1,0:T(8,128)} %constant.108.clone) | copy-start | bytes 193540
  35.0 8.5 %copy-start.7 = (pred[336,640]{1,0:T(8,128)(4,1)S(1)}, pred[336,640]{1,0:T(8,128)(4,1)}, u32[]{:S(2)}) copy-start(pred[336,640]{1,0:T(8,128)(4,1)} %constant.111.clone) | copy-start | bytes 645124
  35.0 8.5 %copy-start.10 = (f32[336,48]{1,0:T(8,128)S(1)}, f32[336,48]{1,0:T(8,128)}, u32[]{:S(2)}) copy-start(f32[336,48]{1,0:T(8,128)} %constant.110.clone) | copy-start | bytes 193540
  45.6 0.7 copy-start.4
  69.5 7.6 %copy-start.2 = (f32[1,320,640]{2,1,0:T(8,128)S(1)}, f32[1,320,640]{2,1,0:T(8,128)}, u32[]{:S(2)}) copy-start(f32[1,320,640]{2,1,0:T(8,128)} %fusion.6) | copy-start | bytes 2457604
  71.8 6.8 %copy-start = (f32[336,640]{1,0:T(8,128)S(1)}, f32[336,640]{1,0:T(8,128)}, u32[]{:S(2)}) copy-start(f32[336,640]{1,0:T(8,128)} %convolution_select_fusion.3) | copy-start | bytes 2580484
  71.8 6.8 %copy-start.5 = (f32[48,640]{1,0:T(8,128)S(1)}, f32[48,640]{1,0:T(8,128)}, u32[]{:S(2)}) copy-start(f32[48,640]{1,0:T(8,128)} %copy-done.4) | copy-start | bytes 368644
  71.8 6.8 %copy-start.8 = (pred[336,640]{1,0:T(8,128)(4,1)S(1)}, pred[336,640]{1,0:T(8,128)(4,1)}, u32[]{:S(2)}) copy-start(pred[336,640]{1,0:T(8,128)(4,1)} %constant.111.clone) | copy-start | bytes 645124
  71.8 6.8 %copy-start.11 = (f32[336,48]{1,0:T(8,128)S(1)}, f32[336,48]{1,0:T(8,128)}, u32[]{:S(2)}) copy-start(f32[336,48]{1,0:T(8,128)} %constant.110.clone) | copy-start | bytes 193540
  71.8 29.9 %all-to-all-start.1 = ((f32[4,20,2688]{2,1,0:T(8,128)}), f32[4,20,2688]{2,1,0:T(8,128)S(1)}, u32[]{:S(2)}, u32[]{:S(2)}) async-start(f32[4,20,2688]{2,1,0:T(8,128)} %copy.36), calls=%async_computation.1 | async-start | bytes 2064384 | tf_op jit(solution)/shard_map/all_to_all | solution.py:411
  77.1 2.4 %copy-start.1 = (f32[1,336,640]{2,1,0:T(8,128)S(1)}, f32[1,336,640]{2,1,0:T(8,128)}, u32[]{:S(2)}) copy-start(f32[1,336,640]{2,1,0:T(8,128)} %fusion.3) | copy-start | bytes 2580484
  146.1 2.4 %collective-permute-start.1 = (f32[16,512]{1,0:T(8,128)S(1)}, f32[16,512]{1,0:T(8,128)S(1)}, u32[]{:S(2)}, u32[]{:S(2)}) collective-permute-start(f32[16,512]{1,0:T(8,128)S(1)} %reshape.79), channel_id=1, source_target_pairs={{1,0},{0,1},{3,2},{2,3},{5,4},{4,5},{7,6},{6,7},{9,8},{8,9},{11,10... | collective-permute-start | bytes 98312 | tf_op jit(solution)/shard_map/ppermute | solution.py:46
  146.2 8.9 %collective-permute-start = (f32[128,512]{1,0:T(8,128)}, f32[128,512]{1,0:T(8,128)S(1)}, u32[]{:S(2)}, u32[]{:S(2)}) collective-permute-start(f32[128,512]{1,0:T(8,128)} %get-tuple-element.34), channel_id=1, source_target_pairs={{2,0},{4,2},{6,4},{8,6},{10,8},{12,10},{14,12},{16,14},{18,16},{20... | collective-permute-start | bytes 786440 | tf_op jit(solution)/shard_map/ppermute | solution.py:46

commit v3 on v2

--- a/solution.py
+++ b/solution.py
@@ -89,7 +89,7 @@
     return regions, head, tail, head_width, width
 
 
-def prep_kernel(n_slab, n_pencil, info, bank, out, end):
+def prep_kernel(n_slab, n_pencil, cut, info, bank, out, rest, end):
     regions, head, tail, head_width, width = regions_of(n_slab, n_pencil)
     step = pl.program_id(0)
     pencil = info[0]
@@ -131,7 +131,8 @@
             for c in range(size // LANES):
                 piece = jnp.where(lanes < LANES - shift, chunks[c], chunks[c + 1])
                 base = r.start + z * size + c * LANES
-                out[0, :, base : base + LANES] = jnp.where(owned, piece, 0.0)
+                target, base = (out, base) if base < cut else (rest, base - cut)
+                target[0, :, base : base + LANES] = jnp.where(owned, piece, 0.0)
 
 
 def split2(value):
@@ -392,24 +393,31 @@
     while inner * inner < n_slab:
         inner *= 2
     outer = n_slab // inner
+    cut = round_up(width // 2, LANES)
     windows = pl.pallas_call(
-        functools.partial(prep_kernel, n_slab, n_pencil),
+        functools.partial(prep_kernel, n_slab, n_pencil, cut),
         grid=(n_slab,),
         in_specs=[smem, pl.BlockSpec(bank.shape, lambda s: (0, 0, 0))],
-        out_specs=pl.BlockSpec(
-            (1, count, width), lambda s: ((s % inner) * outer + s // inner, 0, 0)
-        ),
-        out_shape=jax.ShapeDtypeStruct((n_slab, count, width), F32),
+        out_specs=[
+            pl.BlockSpec((1, count, size), lambda s: ((s % inner) * outer + s // inner, 0, 0))
+            for size in (cut, width - cut)
+        ],
+        out_shape=[
+            jax.ShapeDtypeStruct((n_slab, count, size), F32) for size in (cut, width - cut)
+        ],
         scratch_shapes=[pltpu.VMEM((count, LANES), F32)],
         name="windows",
     )(info, bank)
     near = [[o * inner + i for i in range(inner)] for o in range(outer)]
     far = [[o * inner + i for o in range(outer)] for i in range(inner)]
-    parts = windows.reshape(inner, outer, count, width)
-    parts = lax.all_to_all(parts, "slab", 0, 0, axis_index_groups=near, tiled=True)
-    parts = jnp.sum(parts, axis=0)
-    parts = lax.all_to_all(parts, "slab", 0, 0, axis_index_groups=far, tiled=True)
-    received = jnp.sum(parts, axis=0)
+    received = []
+    for parts in windows:
+        parts = parts.reshape(inner, outer, count, parts.shape[2])
+        parts = lax.all_to_all(parts, "slab", 0, 0, axis_index_groups=near, tiled=True)
+        parts = jnp.sum(parts, axis=0)
+        parts = lax.all_to_all(parts, "slab", 0, 0, axis_index_groups=far, tiled=True)
+        received.append(jnp.sum(parts, axis=0))
+    received = jnp.concatenate(received, axis=1)
 
     padded = round_up(count, 8)
     wide = round_up(padded, 16)

time: 158 us -> 164 us (1.038)
  starting transfers between devices: 13 us -> 17.7 us
  local copies, waits for them, and re-layouts: 21.3 us -> 24.2 us
  matrix products: 16.1 us -> 13.8 us
    all_to_all x1 -> x2, starting transfers between devices: 5.32 us -> 8.91 us  [shards(): lax.all_to_all(parts, 'slab', 0, 0, axis_index_groups=near, tiled=True)]
    all_to_all x1 -> x2, starting transfers between devices: 5.26 us -> 8.62 us  [shards(): lax.all_to_all(parts, 'slab', 0, 0, axis_index_groups=far, tiled=True)]
    ppermute x2, starting transfers between devices: 2.41 us -> 0.13 us  [shifted(): return lax.ppermute(block, axis, route)]
    ppermute x2, waiting for transfers between devices: 3.82 us -> 6.09 us  [shifted(): return lax.ppermute(block, axis, route)]
    all_to_all x1 -> x2, waiting for transfers between devices: 18 us -> 16 us  [shards(): lax.all_to_all(parts, 'slab', 0, 0, axis_index_groups=far, tiled=True)]
    reshape x1 -> x2, local copies, waits for them, and re-layouts: 4.78 us -> 6.69 us  [shards(): parts = parts.reshape(inner, outer, count, parts.shape[2])]
    reduce_sum x1 -> x2, local copies, waits for them, and re-layouts: 2.27 us -> 3.92 us  [shards(): parts = jnp.sum(parts, axis=0)]
    unnamed x40 -> x54, local copies, waits for them, and re-layouts: 6.93 us -> 7.76 us
  transfers between devices with their start and end apart: 4 -> 6, of which waited for: 3 -> 6; matrix products, arithmetic and copies ran while one was open for 18% -> 21% of each run, Pallas kernels for 0% -> 0%
where the time goes in v3:
time: 164 us; the launch traced here: 163 us
  Pallas kernels  50.7 us (31%)
  waiting for transfers between devices  41.3 us (25%)
  local copies, waits for them, and re-layouts  24.2 us (15%)
  starting transfers between devices  17.7 us (11%)
  matrix products  13.8 us (8%)
  other arithmetic  13.7 us (8%)
  between operations  1.69 us (1%)
    pallas_call x1, Pallas kernels, shards(): pl.pallas_call(fine_kernel, grid=(nz, ny), in_specs=[pl.BlockSpec((count,...  29.5 us
    all_to_all x2, waiting for transfers between devices, shards(): lax.all_to_all(parts, 'slab', 0, 0, axis_index_groups=near, tiled=True)  19.2 us
    all_to_all x2, waiting for transfers between devices, shards(): lax.all_to_all(parts, 'slab', 0, 0, axis_index_groups=far, tiled=True)  16 us
    dot_general x6, matrix products, packed_weights(): part = jnp.dot(jnp.asarray(pick), wide, precision=HI)  9.95 us
    pallas_call x1, Pallas kernels, shards(): pl.pallas_call(functools.partial(prep_kernel, n_slab, n_pencil, cut), gri...  9.84 us
    all_to_all x2, starting transfers between devices, shards(): lax.all_to_all(parts, 'slab', 0, 0, axis_index_groups=near, tiled=True)  8.91 us
    all_to_all x2, starting transfers between devices, shards(): lax.all_to_all(parts, 'slab', 0, 0, axis_index_groups=far, tiled=True)  8.62 us
    unnamed x54, local copies, waits for them, and re-layouts  7.76 us
  transfers between devices with their start and end apart: 6, of which 6 were waited for; matrix products, arithmetic and copies ran while one was open for 21% of the time, Pallas kernels for 0%

profile of v3, /device:TPU:0, one launch (start us, length us, event | category | flops | bytes accessed | tf_op | source)
XLA Modules:
  0.0 163.1 jit_solution(3269667994214506572)
XLA Ops:
  1.3 6.2 %copy.36.bank = f32[1,20,74898]{2,1,0:T(8,128)} copy(f32[1,20,74898]{2,0,1:T(1,128)} %param.25) | data formatting | bytes 11983680 | tf_op args[4]
  8.1 9.8 %windows.1 = (f32[16,20,1408]{2,1,0:T(8,128)}, f32[16,20,1280]{2,1,0:T(8,128)}) custom-call(s32[7]{0:T(128)} %pad_add_fusion.1.info, f32[1,20,74898]{2,1,0:T(8,128)} %copy.36.bank), custom_call_target="tpu_custom_call" | custom-call | tf_op jit(solution)/shard_map/windows/pallas_call | solution.py:397
  18.0 3.3 %copy.39 = f32[4,4,20,1280]{3,1,2,0:T(4,128)} copy(f32[4,4,20,1280]{3,2,1,0:T(8,128)} %bitcast.98) | data formatting | bytes 3276800 | tf_op jit(solution)/shard_map/reshape | solution.py:415
  21.3 5.3 %all-to-all-start.2 = ((f32[4,4,20,1280]{3,1,2,0:T(4,128)}), f32[4,4,20,1280]{3,1,2,0:T(4,128)S(1)}, u32[]{:S(2)}, u32[]{:S(2)}) async-start(f32[4,4,20,1280]{3,1,2,0:T(4,128)} %copy.39), calls=%async_computation.2 | async-start | bytes 3276800 | tf_op jit(solution)/shard_map/all_to_all | solution.py:416
  26.7 3.3 %copy.37 = f32[4,4,20,1408]{3,1,2,0:T(4,128)} copy(f32[4,4,20,1408]{3,2,1,0:T(8,128)} %bitcast.97) | data formatting | bytes 3604480 | tf_op jit(solution)/shard_map/reshape | solution.py:415
  35.7 10.9 %all-to-all-done.2 = f32[4,4,20,1280]{3,1,2,0:T(4,128)S(1)} async-done(((f32[4,4,20,1280]{3,1,2,0:T(4,128)}), f32[4,4,20,1280]{3,1,2,0:T(4,128)S(1)}, u32[]{:S(2)}, u32[]{:S(2)}) %all-to-all-start.2) | async-done | bytes 1638432 | tf_op jit(solution)/shard_map/all_to_all | solution.py:416
  46.6 3.6 %all-to-all-start = ((f32[4,4,20,1408]{3,1,2,0:T(4,128)}), f32[4,4,20,1408]{3,1,2,0:T(4,128)S(1)}, u32[]{:S(2)}, u32[]{:S(2)}) async-start(f32[4,4,20,1408]{3,1,2,0:T(4,128)} %copy.37), calls=%async_computation | async-start | bytes 3604480 | tf_op jit(solution)/shard_map/all_to_all | solution.py:416
  52.6 1.9 %convolution_select_fusion.1 = f32[336,640]{1,0:T(8,128)S(1)} fusion(pred[336,640]{1,0:T(8,128)(4,1)} %constant.109.clone, f32[336,48]{1,0:T(8,128)} %constant.108.clone, f32[48,640]{1,0:T(8,128)S(1)} %fusion.16), kind=kOutput, calls=%fused_computation.13 | convolution fusion | flops 124078080 | bytes 1262592 | tf_op jit(solution)/shard_map/dot_general | solution.py:374
  54.4 2.8 %fusion.3 = f32[1,336,640]{2,1,0:T(8,128)} fusion(f32[336,640]{1,0:T(8,128)S(1)} %convolution_select_fusion.1, pred[336,640]{1,0:T(8,128)(4,1)} %constant.111.clone, f32[336,48]{1,0:T(8,128)} %constant.110.clone, f32[48,640]{1,0:T(8,128)S(1)} %fusion.16), kind=kOutput, calls=%fused_computation.12 | convolution fusion | flops 124293120 | bytes 2122752 | tf_op jit(solution)/shard_map/dot_general | solution.py:374
  58.2 1.7 %convolution_select_fusion.3 = f32[336,640]{1,0:T(8,128)} fusion(pred[336,640]{1,0:T(8,128)(4,1)S(1)} %copy-done.12, f32[336,48]{1,0:T(8,128)S(1)} %copy-done.14, f32[48,640]{1,0:T(8,128)S(1)} %fusion.12), kind=kOutput, calls=%fused_computation.17 | convolution fusion | flops 124078080 | bytes 1262592 | tf_op jit(solution)/shard_map/dot_general | solution.py:374
  61.2 1.9 %copy.40 = f32[4,20,1280]{2,1,0:T(8,128)} copy(f32[4,20,1280]{2,0,1:T(4,128)} %reduce_sum.38) | data formatting | bytes 819200 | tf_op jit(solution)/shard_map/reduce_sum | solution.py:417
  63.1 8.2 %all-to-all-done = f32[4,4,20,1408]{3,1,2,0:T(4,128)S(1)} async-done(((f32[4,4,20,1408]{3,1,2,0:T(4,128)}), f32[4,4,20,1408]{3,1,2,0:T(4,128)S(1)}, u32[]{:S(2)}, u32[]{:S(2)}) %all-to-all-start) | async-done | bytes 1802272 | tf_op jit(solution)/shard_map/all_to_all | solution.py:416
  71.4 5.0 %all-to-all-start.3 = ((f32[4,20,1280]{2,1,0:T(8,128)}), f32[4,20,1280]{2,1,0:T(8,128)S(1)}, u32[]{:S(2)}, u32[]{:S(2)}) async-start(f32[4,20,1280]{2,1,0:T(8,128)} %copy.40), calls=%async_computation.3 | async-start | bytes 983040 | tf_op jit(solution)/shard_map/all_to_all | solution.py:418
  76.5 2.0 %fusion.5 = f32[1,336,640]{2,1,0:T(8,128)S(1)} fusion(f32[336,640]{1,0:T(8,128)S(1)} %copy-done, pred[336,640]{1,0:T(8,128)(4,1)} %constant.111.clone, f32[336,48]{1,0:T(8,128)} %constant.110.clone, f32[48,640]{1,0:T(8,128)S(1)} %copy-done.10), kind=kOutput, calls=%fused_computation.16 | convolution fusion | flops 124293120 | bytes 2122752 | tf_op jit(solution)/shard_map/dot_general | solution.py:374
  81.5 2.0 %copy.38 = f32[4,20,1408]{2,1,0:T(8,128)} copy(f32[4,20,1408]{2,0,1:T(4,128)} %reduce_sum.36) | data formatting | bytes 901120 | tf_op jit(solution)/shard_map/reduce_sum | solution.py:417
  83.5 5.9 %all-to-all-done.3 = f32[4,20,1280]{2,1,0:T(8,128)S(1)} async-done(((f32[4,20,1280]{2,1,0:T(8,128)}), f32[4,20,1280]{2,1,0:T(8,128)S(1)}, u32[]{:S(2)}, u32[]{:S(2)}) %all-to-all-start.3) | async-done | bytes 409632 | tf_op jit(solution)/shard_map/all_to_all | solution.py:418
  90.2 3.7 %all-to-all-start.1 = ((f32[4,20,1408]{2,1,0:T(8,128)}), f32[4,20,1408]{2,1,0:T(8,128)S(1)}, u32[]{:S(2)}, u32[]{:S(2)}) async-start(f32[4,20,1408]{2,1,0:T(8,128)} %copy.38), calls=%async_computation.1 | async-start | bytes 1081344 | tf_op jit(solution)/shard_map/all_to_all | solution.py:418
  96.1 1.7 %pad_maximum_fusion.weights = bf16[2,336,1920]{2,1,0:T(8,128)(2,1)} fusion(bf16[2,336,640]{2,1,0:T(8,128)(2,1)S(1)} %copy-done.2, bf16[2,336,640]{2,1,0:T(8,128)(2,1)S(1)} %get-tuple-element.41), kind=kLoop, calls=%fused_computation | loop fusion | flops 7741440 | bytes 4300800 | tf_op jit(solution)/shard_map/concatenate | solution.py:380
  97.9 10.2 %all-to-all-done.1 = f32[4,20,1408]{2,1,0:T(8,128)S(1)} async-done(((f32[4,20,1408]{2,1,0:T(8,128)}), f32[4,20,1408]{2,1,0:T(8,128)S(1)}, u32[]{:S(2)}, u32[]{:S(2)}) %all-to-all-start.1) | async-done | bytes 450592 | tf_op jit(solution)/shard_map/all_to_all | solution.py:418
  108.8 4.7 %coarse.1 = f32[32,2048]{1,0:T(8,128)} custom-call(s32[2]{0:T(128)} %pad_add_fusion.info, f32[20,2688]{1,0:T(8,128)} %pad_maximum_fusion.4.received, bf16[32,224]{1,0:T(8,128)(2,1)} %get-tuple-element.70.w_high, bf16[32,224]{1,0:T(8,128)(2,1)} %get-tuple-element.69.w_low), custom_call_target="tpu_custom_call" | custom-call | tf_op jit(solution)/shard_map/coarse/pallas_call | solution.py:434
  115.3 6.7 %middle.1 = f32[20,4,32,128]{3,2,1,0:T(8,128)} custom-call(s32[1]{0:T(128)} %bitcast.info, f32[20,2,16,64]{3,2,1,0:T(8,128)} %reshape.81.upper, f32[20,4,32,128]{3,2,1,0:T(8,128)} %noise.2, bf16[2,320,1920]{2,1,0:T(8,128)(2,1)} %pad_maximum_fusion.1.weights), custom_call_target="tpu_custom_call" | custom-call | tf_op jit(solution)/shard_map/middle/pallas_call | solution.py:451
  121.9 29.5 %fine.1 = (f32[16,128,512]{2,1,0:T(8,128)}, f32[8,128,512]{2,1,0:T(8,128)}, f32[16,64,512]{2,1,0:T(8,128)}, f32[128,512]{1,0:T(8,128)}, f32[4,2,8,512]{3,2,1,0:T(8,128)}) custom-call(f32[20,4,32,128]{3,2,1,0:T(8,128)} %middle.1, f32[20,8,64,256]{3,2,1,0:T(8,128)} %noise.3, bf16[2,336,1920]{2,1,0:T(8,128)(2,1)} %pad_maximum_fusion.weights), custom_call_target="tpu_custom_call" | custom-call | tf_op jit(solution)/shard_map/fine/pallas_call | solution.py:478
  154.7 1.8 %scatter-add.9 = f32[16,64,512]{2,1,0:T(8,128)} dynamic-update-slice(f32[16,64,512]{2,1,0:T(8,128)} %get-tuple-element.39, f32[16,1,512]{2,1,0:T(1,128)S(1)} %reshape_add_fusion, s32[]{:T(128)} %constant.96.clone.1, s32[]{:T(128)} %constant.102.clone.1, s32[]{:T(128)} %constant.96.clone.1) | dynamic-update-slice | bytes 65540 | tf_op jit(solution)/shard_map/scatter-add | solution.py:509
  156.4 5.0 %collective-permute-done = f32[128,512]{1,0:T(8,128)S(1)} collective-permute-done((f32[128,512]{1,0:T(8,128)}, f32[128,512]{1,0:T(8,128)S(1)}, u32[]{:S(2)}, u32[]{:S(2)}) %collective-permute-start) | collective-permute-done | bytes 262176 | tf_op jit(solution)/shard_map/ppermute | solution.py:46
  (89 shorter events, 24.4 us)
Async XLA Ops:
  1.3 6.2 %copy-start.25 = (s32[16]{0:T(128)S(1)}, s32[16]{0:T(128)}, u32[]{:S(2)}) copy-start(s32[16]{0:T(128)} %param.21) | copy-start | bytes 196
  21.3 5.3 %copy-start.11 = (f32[8,20,20]{2,0,1:T(8,128)S(1)}, f32[8,20,20]{2,0,1:T(8,128)}, u32[]{:S(2)}) copy-start(f32[8,20,20]{2,0,1:T(8,128)} %param.23) | copy-start | bytes 38404
  21.3 25.3 %all-to-all-start.2 = ((f32[4,4,20,1280]{3,1,2,0:T(4,128)}), f32[4,4,20,1280]{3,1,2,0:T(4,128)S(1)}, u32[]{:S(2)}, u32[]{:S(2)}) async-start(f32[4,4,20,1280]{3,1,2,0:T(4,128)} %copy.39), calls=%async_computation.2 | async-start | bytes 3276800 | tf_op jit(solution)/shard_map/all_to_all | solution.py:416
  26.7 4.3 %copy-start.24 = (f32[20,20]{1,0:T(8,128)S(1)}, f32[20,20]{1,0:T(8,128)}, u32[]{:S(2)}) copy-start(f32[20,20]{1,0:T(8,128)} %constant.103.clone) | copy-start | bytes 4804
  26.7 4.4 %copy-start.5 = (f32[60,640]{1,0:T(8,128)S(1)}, f32[60,640]{1,0:T(8,128)}, u32[]{:S(2)}) copy-start(f32[60,640]{1,0:T(8,128)} %constant.104.clone) | copy-start | bytes 460804
  26.7 4.7 %copy-start.13 = (pred[320,640]{1,0:T(32,128)(4,1)S(1)}, pred[320,640]{1,0:T(32,128)(4,1)}, u32[]{:S(2)}) copy-start(pred[320,640]{1,0:T(32,128)(4,1)} %constant.106.clone) | copy-start | bytes 614404
  26.7 4.7 %copy-start.15 = (f32[320,40]{1,0:T(8,128)S(1)}, f32[320,40]{1,0:T(8,128)}, u32[]{:S(2)}) copy-start(f32[320,40]{1,0:T(8,128)} %constant.105.clone) | copy-start | bytes 153604
  46.6 24.8 %all-to-all-start = ((f32[4,4,20,1408]{3,1,2,0:T(4,128)}), f32[4,4,20,1408]{3,1,2,0:T(4,128)S(1)}, u32[]{:S(2)}, u32[]{:S(2)}) async-start(f32[4,4,20,1408]{3,1,2,0:T(4,128)} %copy.37), calls=%async_computation | async-start | bytes 3604480 | tf_op jit(solution)/shard_map/all_to_all | solution.py:416
  50.2 7.0 %copy-start.6 = (f32[60,640]{1,0:T(8,128)S(1)}, f32[60,640]{1,0:T(8,128)}, u32[]{:S(2)}) copy-start(f32[60,640]{1,0:T(8,128)} %constant.104.clone) | copy-start | bytes 460804
  50.2 7.0 %copy-start.18 = (f32[24,20]{1,0:T(8,128)S(1)}, f32[24,20]{1,0:T(8,128)}, u32[]{:S(2)}) copy-start(f32[24,20]{1,0:T(8,128)} %get-tuple-element.45) | copy-start | bytes 5764
  50.2 7.0 %copy-start.19 = (f32[24,20]{1,0:T(8,128)S(1)}, f32[24,20]{1,0:T(8,128)}, u32[]{:S(2)}) copy-start(f32[24,20]{1,0:T(8,128)} %get-tuple-element.50) | copy-start | bytes 5764
  50.2 7.0 %copy-start.20 = (f32[24,20]{1,0:T(8,128)S(1)}, f32[24,20]{1,0:T(8,128)}, u32[]{:S(2)}) copy-start(f32[24,20]{1,0:T(8,128)} %get-tuple-element.51) | copy-start | bytes 5764
  50.2 7.0 %copy-start.21 = (f32[24,20]{1,0:T(8,128)S(1)}, f32[24,20]{1,0:T(8,128)}, u32[]{:S(2)}) copy-start(f32[24,20]{1,0:T(8,128)} %get-tuple-element.52) | copy-start | bytes 5764
  51.2 7.1 %copy-start.12 = (pred[336,640]{1,0:T(8,128)(4,1)S(1)}, pred[336,640]{1,0:T(8,128)(4,1)}, u32[]{:S(2)}) copy-start(pred[336,640]{1,0:T(8,128)(4,1)} %constant.109.clone) | copy-start | bytes 645124
  51.2 7.1 %copy-start.14 = (f32[336,48]{1,0:T(8,128)S(1)}, f32[336,48]{1,0:T(8,128)}, u32[]{:S(2)}) copy-start(f32[336,48]{1,0:T(8,128)} %constant.108.clone) | copy-start | bytes 193540
  60.0 16.4 %copy-start.17 = (f32[32,32]{1,0:T(8,128)S(1)}, f32[32,32]{1,0:T(8,128)}, u32[]{:S(2)}) copy-start(f32[32,32]{1,0:T(8,128)} %pad.13) | copy-start | bytes 12292
  61.2 15.3 %copy-start = (f32[336,640]{1,0:T(8,128)S(1)}, f32[336,640]{1,0:T(8,128)}, u32[]{:S(2)}) copy-start(f32[336,640]{1,0:T(8,128)} %convolution_select_fusion.3) | copy-start | bytes 2580484
  61.2 15.3 %copy-start.10 = (f32[48,640]{1,0:T(8,128)S(1)}, f32[48,640]{1,0:T(8,128)}, u32[]{:S(2)}) copy-start(f32[48,640]{1,0:T(8,128)} %copy-done.9) | copy-start | bytes 368644
  71.4 18.0 %all-to-all-start.3 = ((f32[4,20,1280]{2,1,0:T(8,128)}), f32[4,20,1280]{2,1,0:T(8,128)S(1)}, u32[]{:S(2)}, u32[]{:S(2)}) async-start(f32[4,20,1280]{2,1,0:T(8,128)} %copy.40), calls=%async_computation.3 | async-start | bytes 983040 | tf_op jit(solution)/shard_map/all_to_all | solution.py:418
  81.5 13.0 %copy-start.3 = (bf16[2,320,640]{2,1,0:T(8,128)(2,1)S(1)}, bf16[2,320,640]{2,1,0:T(8,128)(2,1)}, u32[]{:S(2)}) copy-start(bf16[2,320,640]{2,1,0:T(8,128)(2,1)} %get-tuple-element.43) | copy-start | bytes 2457604
  81.5 13.0 %copy-start.4 = (bf16[2,320,640]{2,1,0:T(8,128)(2,1)S(1)}, bf16[2,320,640]{2,1,0:T(8,128)(2,1)}, u32[]{:S(2)}) copy-start(bf16[2,320,640]{2,1,0:T(8,128)(2,1)} %get-tuple-element.44) | copy-start | bytes 2457604
  90.2 17.8 %all-to-all-start.1 = ((f32[4,20,1408]{2,1,0:T(8,128)}), f32[4,20,1408]{2,1,0:T(8,128)S(1)}, u32[]{:S(2)}, u32[]{:S(2)}) async-start(f32[4,20,1408]{2,1,0:T(8,128)} %copy.38), calls=%async_computation.1 | async-start | bytes 1081344 | tf_op jit(solution)/shard_map/all_to_all | solution.py:418
  152.4 1.3 collective-permute-start.1
  152.5 8.9 %collective-permute-start = (f32[128,512]{1,0:T(8,128)}, f32[128,512]{1,0:T(8,128)S(1)}, u32[]{:S(2)}, u32[]{:S(2)}) collective-permute-start(f32[128,512]{1,0:T(8,128)} %get-tuple-element.38), channel_id=1, source_target_pairs={{2,0},{4,2},{6,4},{8,6},{10,8},{12,10},{14,12},{16,14},{18,16},{20... | collective-permute-start | bytes 786440 | tf_op jit(solution)/shard_map/ppermute | solution.py:46
  (8 other events, 16.8 us)
